TPU v7x, 32 devices: a whole 2x2x4 slice. The times are simulated.
32 devices in a mesh: batch: 8 (over z, y), doc: 4 (over x, core).
Axes of the slice: x: 2, y: 2, z: 4, core: 2. Of those that a mesh axis runs over, the one named last changes fastest.
Arguments:
- hidden_in: bfloat16 [8, 4, 288, 768], P('batch', 'doc'), may hold values from -6 to 6
- segments: int32 [8, 4, 288], P('batch', 'doc'), may hold values from 0 to 3, as said below
- mask_pos: int32 [8, 4, 4, 8], P('batch', 'doc'), may hold values from 0 to 287, as said below
- target_ids: int32 [8, 4, 8], replicated, may hold values from 0 to 8191
- query_emb: float32 [8, 4, 128], P('batch', None, 'doc'), may hold values from -6 to 6
- doc_emb: float32 [8, 4, 4, 128], P('batch', 'doc'), may hold values from -0.9 to 0.9
- qkv_weight: bfloat16 [768, 2304], replicated, may hold values from -0.21875 to 0.21875
- query_bias: float32 [768], replicated, may hold values from -3 to 3
- value_bias: float32 [768], replicated, may hold values from -3 to 3
- out_weight: bfloat16 [768, 768], replicated, may hold values from -1.25 to 1.25
- out_bias: float32 [768], replicated, may hold values from -3 to 3
- gain_one: float32 [768], replicated, may hold values from 0.5 to 1.5
- shift_one: float32 [768], replicated, may hold values from -2 to 2
- up_weight: bfloat16 [768, 3072], replicated, may hold values from -0.21875 to 0.21875
- up_bias: float32 [3072], replicated, may hold values from -3 to 3
- down_weight: bfloat16 [3072, 768], replicated, may hold values from -0.21875 to 0.21875
- down_bias: float32 [768], replicated, may hold values from -3 to 3
- gain_two: float32 [768], replicated, may hold values from 0.5 to 1.5
- shift_two: float32 [768], replicated, may hold values from -2 to 2
- vocab: bfloat16 [8192, 768], P('batch'), may hold values from -0.4375 to 0.4375
Outputs:
- block_out: bfloat16 [8, 4, 288, 768], P('batch', 'doc')
- loss: float32 [8, 4], P('batch')
- grad_in: bfloat16 [8, 4, 288, 768], P('batch', 'doc')
- grad_query: float32 [8, 4, 128], P('batch', None, 'doc')
- grad_qkv_weight: float32 [768, 2304], P('batch')
- grad_query_bias: float32 [768], P('batch')
- grad_value_bias: float32 [768], P('batch')
- grad_out_weight: float32 [768, 768], P('batch')
- grad_out_bias: float32 [768], P('batch')
- grad_gain_one: float32 [768], P('batch')
- grad_shift_one: float32 [768], P('batch')
- grad_up_weight: float32 [768, 3072], P('batch')
- grad_up_bias: float32 [3072], P('batch')
- grad_down_weight: float32 [3072, 768], P('batch')
- grad_down_bias: float32 [768], P('batch')
- grad_gain_two: float32 [768], P('batch')
- grad_shift_two: float32 [768], P('batch')
Inputs may be any that keep to these rules, and one draw needn't show every extreme that they name: `segments`: in each sequence the segment numbers never fall and every one of 0 to 3 occurs; segment q holds pair q. `mask_pos`: the 8 positions of pair q rise strictly and lie in segment q of their sequence.
All inputs are finite; a program needn't handle non-finite values.
Results may differ from a plain program's by a relative error of at most 0.025.
Values may be sent and summed in bfloat16 or wider, within the bound.
A program may use at most 128 MiB of HBM per device.

v0:
```python
from functools import partial
import itertools
import math

import jax
import jax.numpy as jnp
from jax import lax
from jax.experimental import pallas as pl
from jax.experimental.pallas import tpu as pltpu
from jax.sharding import PartitionSpec as P

HEAD_DIM = 64
MESH = pl.DeviceIdType.MESH
VMEM_BYTES = 64000000


class Spot:
    def __init__(self):
        self.at = {"batch": lax.axis_index("batch"), "doc": lax.axis_index("doc")}

    def mine(self, key):
        axis, k = key
        return lax.rem(self.at[axis] // (1 << k), 2)

    def peer(self, key):
        axis, k = key
        moved = dict(self.at)
        moved[axis] = self.at[axis] + (1 - 2 * self.mine(key)) * (1 << k)
        return (moved["batch"], moved["doc"])


def mesh_keys(nb, nd):
    batch = [("batch", k) for k in range(nb.bit_length() - 1)]
    doc = [("doc", k) for k in range(nd.bit_length() - 1)]
    return batch, doc


class Piece:
    def __init__(self, mat, col, rows, cols, lead, halve, both, spread):
        self.mat, self.col, self.rows, self.cols = mat, col, rows, cols
        self.lead, self.halve, self.both, self.spread = lead, halve, both, spread
        self.tile = (rows, cols)
        self.steps = (
            [("halve", key) for key in halve]
            + [("both", key) for key in both]
            + [("spread", key) for key in spread]
            + [("twin", ("doc", 0))]
        )
        self.width = cols * 2 ** len(spread)

    def buffers(self):
        two = [(2,) * (len(self.lead) - i - 1) + self.tile for i in range(len(self.halve))]
        two += [self.tile] * len(self.both)
        wide = (2,) * len(self.spread) + self.tile
        return [(2,) * len(self.lead) + self.tile] + two + [wide, wide]

    def bytes(self, i):
        kind, key = self.steps[i]
        unit = self.rows * self.cols * 2
        if kind == "halve":
            return unit * 2 ** (len(self.lead) - i - 1)
        return unit * (2 if kind == "twin" and self.spread else 1)


def plan_pieces(nb, nd, mats):
    batch, doc = mesh_keys(nb, nd)
    across = doc[1:]
    pieces = []
    for m, (rows, cols) in enumerate(mats):
        first = across[:1] if len(across) == 1 else []
        col = 0
        if first and cols % 256 == 0 and m == 0 or first and cols > 1024:
            wide = cols // 2 // 256 * 256 if m else 256
            chunk = 256 if wide % 512 else 512
            for _ in range(wide // chunk):
                pieces.append(
                    Piece(m, col, rows, chunk // 2, first + batch[::-1], first + batch, [], first)
                )
                col += chunk
        while col < cols:
            chunk = min(cols - col, 512)
            pieces.append(Piece(m, col, rows, chunk, batch[::-1], batch, across, []))
            col += chunk
    return pieces


def exchange_order(pieces, ready, topology):
    free = {}
    clock = [(ready[i], i, 0) for i in range(len(pieces))]
    done = []
    while clock:
        clock.sort()
        at, i, step = clock.pop(0)
        key = pieces[i].steps[step][1]
        link, weight, rate = topology[key]
        start = max(at, free.get(link, 0.0))
        end = start + pieces[i].bytes(step) * weight / rate
        free[link] = end
        done.append((end + 1.5, i, step))
        if step + 1 < len(pieces[i].steps):
            clock.append((end + 2.0, i, step + 1))
    return [(i, step) for _, i, step in sorted(done)]


class Flow:
    def __init__(self, piece, bufs, send, recv, base, spot):
        self.p, self.bufs, self.send, self.recv, self.base, self.spot = piece, bufs, send, recv, base, spot
        self.live = {}
        self.copies = []

    @property
    def grad(self):
        return self.bufs[0]

    def index(self, fixed):
        return tuple(fixed.get(key, slice(None)) for key in self.p.lead)

    def start(self, step):
        kind, key = self.p.steps[step]
        mine = self.spot.mine(key)
        n = len(self.p.halve) + len(self.p.both)
        if kind == "halve":
            src = self.bufs[0].at[self.index({**self.live, key: 1 - mine})]
            dst = self.bufs[1 + step]
        elif kind == "both":
            src = self.bufs[0].at[self.index(self.live)]
            dst = self.bufs[1 + step]
        elif kind == "spread":
            src = self.bufs[n + 1].at[mine]
            dst = self.bufs[n + 1].at[mine]
        else:
            src = self.bufs[n + 1]
            dst = self.bufs[n + 2]
        copy = pltpu.make_async_remote_copy(
            src_ref=src,
            dst_ref=dst,
            send_sem=self.send.at[self.base + step],
            recv_sem=self.recv.at[self.base + step],
            device_id=self.spot.peer(key),
            device_id_type=MESH,
        )
        copy.start()
        self.copies.append(copy)

    def finish(self, step):
        kind, key = self.p.steps[step]
        copy = self.copies[step]
        if kind == "both":
            copy.wait()
        else:
            copy.wait_recv()
        n = len(self.p.halve) + len(self.p.both)
        if kind in ("halve", "both"):
            if kind == "halve":
                self.live[key] = self.spot.mine(key)
            got = self.bufs[1 + step]
            free = [k for k in self.p.lead if k not in self.live]
            last = step + 1 == n
            for pick in itertools.product(range(2), repeat=len(free)):
                at = self.index({**self.live, **dict(zip(free, pick))})
                total = self.bufs[0][at] + got[pick]
                if last:
                    self.bufs[n + 1][tuple(self.spot.mine(k) for k in self.p.spread)] = total
                else:
                    self.bufs[0][at] = total

    def drain(self):
        for step, copy in enumerate(self.copies):
            if self.p.steps[step][0] != "both":
                copy.wait_send()


def link_table(nb, nd):
    batch, doc = mesh_keys(nb, nd)
    table = {key: (key, 2.0, 91e3) for key in batch + doc}
    table[("doc", 0)] = ("twin", 1.0, 450e3)
    if (nb, nd) == (8, 4):
        table[("batch", 1)] = ("z", 2.0, 91e3)
        table[("batch", 2)] = ("z", 4.0, 91e3)
    return table


def reduce_kernel(pieces, halves, order, n_mats, *refs):
    mats, refs = refs[:n_mats], refs[n_mats:]
    vec, refs = refs[0], refs[1:]
    outs, refs = refs[:n_mats], refs[n_mats:]
    vec_out, refs = refs[0], refs[1:]
    spot = Spot()
    nb, nd = lax.axis_size("batch"), lax.axis_size("doc")
    batch, doc = mesh_keys(nb, nd)
    keys = batch + doc
    bufs = []
    for p in pieces:
        k = len(p.buffers())
        bufs.append(refs[:k])
        refs = refs[k:]
    vec_send, vec_recv = refs[:2]
    send, recv, twin_send, twin_recv, vs, vr = refs[2:]

    barrier = pltpu.get_barrier_semaphore()
    for key in keys:
        pl.semaphore_signal(barrier, inc=1, device_id=spot.peer(key), device_id_type=MESH)
    pl.semaphore_wait(barrier, len(keys))

    core = spot.mine(("doc", 0))
    twin = spot.peer(("doc", 0))
    flows = []
    base = 0
    twins = []
    for i, p in enumerate(pieces):
        flow = Flow(p, bufs[i], send, recv, base, spot)
        base += len(p.steps)
        flows.append(flow)
        half = halves[p.mat]
        copies = []
        for j in range(2 ** len(p.spread)):
            cols = pl.ds(pl.multiple_of((1 - core) * half + p.col + j * p.cols, 128), p.cols)
            dst = flow.grad.at[j] if p.spread else flow.grad
            lead = (slice(None),) * len(batch)
            copy = pltpu.make_async_remote_copy(
                src_ref=mats[p.mat].at[lead + (slice(None), cols)],
                dst_ref=dst,
                send_sem=twin_send.at[2 * i + j],
                recv_sem=twin_recv.at[2 * i + j],
                device_id=twin,
                device_id_type=MESH,
            )
            copy.start()
            copies.append(copy)
        twins.append(copies)

    vec_now = vec[...]
    vec_copies = []

    def vec_step(i):
        vec_send[i] = vec_now.astype(jnp.bfloat16)
        copy = pltpu.make_async_remote_copy(
            src_ref=vec_send.at[i],
            dst_ref=vec_recv.at[i],
            send_sem=vs.at[i],
            recv_sem=vr.at[i],
            device_id=spot.peer(keys[i]),
            device_id_type=MESH,
        )
        copy.start()
        vec_copies.append(copy)

    vec_step(0)
    for i, p in enumerate(pieces):
        half = halves[p.mat]
        for j, copy in enumerate(twins[i]):
            copy.wait()
            cols = pl.ds(pl.multiple_of(core * half + p.col + j * p.cols, 128), p.cols)
            for pick in itertools.product(range(2), repeat=len(batch)):
                at = ((j,) if p.spread else ()) + pick
                flows[i].grad[at] = flows[i].grad[at] + mats[p.mat][pick + (slice(None), cols)]
        flows[i].start(0)
        if i + 1 < len(keys):
            vec_copies[i].wait()
            vec_now = vec_now + vec_recv[i].astype(jnp.float32)
            vec_step(i + 1)
    for i in range(len(vec_copies), len(keys) + 1):
        vec_copies[i - 1].wait()
        vec_now = vec_now + vec_recv[i - 1].astype(jnp.float32)
        if i < len(keys):
            vec_step(i)
    vec_out[...] = vec_now

    for i, step in order:
        flows[i].finish(step)
        p = pieces[i]
        if step + 1 < len(p.steps):
            flows[i].start(step + 1)
        else:
            half = halves[p.mat]
            for side, buf in ((core, bufs[i][-2]), (1 - core, bufs[i][-1])):
                for j in range(2 ** len(p.spread)):
                    cols = pl.ds(pl.multiple_of(side * half + p.col + j * p.cols, 128), p.cols)
                    outs[p.mat][:, cols] = buf[j] if p.spread else buf[...]
    for flow in flows:
        flow.drain()


def reduce_params(mats, vectors, nb, nd):
    batch, doc = mesh_keys(nb, nd)
    shares = [(m.shape[0] // nb, m.shape[1]) for m in mats]
    halves = [c // 2 for _, c in shares]
    pieces = plan_pieces(nb, nd, [(r, c // 2) for r, c in shares])
    order = exchange_order(pieces, [3.0 * i for i in range(len(pieces))], link_table(nb, nd))
    keys = batch + doc
    scratch = []
    for p in pieces:
        scratch += [pltpu.VMEM(shape, jnp.bfloat16) for shape in p.buffers()]
    scratch += [pltpu.VMEM((len(keys),) + vectors.shape, jnp.bfloat16)] * 2
    steps = sum(len(p.steps) for p in pieces)
    dma = pltpu.SemaphoreType.DMA
    scratch += [dma((steps,)), dma((steps,)), dma((2 * len(pieces),)), dma((2 * len(pieces),))]
    scratch += [dma((len(keys),)), dma((len(keys),))]
    vm = pl.BlockSpec(memory_space=pltpu.VMEM)
    return pl.pallas_call(
        partial(reduce_kernel, pieces, halves, order, len(mats)),
        out_shape=[jax.ShapeDtypeStruct(s, jnp.bfloat16) for s in shares]
        + [jax.ShapeDtypeStruct(vectors.shape, jnp.float32)],
        in_specs=[vm] * (len(mats) + 1),
        out_specs=[vm] * (len(mats) + 1),
        scratch_shapes=scratch,
        compiler_params=pltpu.CompilerParams(
            collective_id=0, has_side_effects=True, vmem_limit_bytes=VMEM_BYTES
        ),
    )(*[m.reshape((2,) * len(batch) + (m.shape[0] // nb, m.shape[1])) for m in mats], vectors)


def combined_all(x, axis, combine):
    everything = jax.tree.map(lambda part: lax.all_gather(part, axis), x)
    leading = jax.tree.map(lambda part: part[0], everything)

    def hop(k, so_far):
        return combine(so_far, jax.tree.map(lambda part: part[k], everything))

    return lax.fori_loop(1, lax.axis_size(axis), hop, leading)


def norm_rows(values, gain, shift):
    centre = jnp.mean(values, -1, keepdims=True)
    centred = values - centre
    spread = jnp.mean(centred * centred, -1, keepdims=True)
    return centred * lax.rsqrt(spread + 1e-06) * gain + shift


def lse_pair(earlier, later):
    maxima = jnp.maximum(earlier[0], later[0])
    totals = earlier[1] * jnp.exp(earlier[0] - maxima) + later[1] * jnp.exp(later[0] - maxima)
    return (maxima, totals)


def vocab_pair(earlier, later):
    return lse_pair(earlier[:2], later[:2]) + (earlier[2] + later[2],)


def place_rows(places, grads, seq_len):
    return jnp.zeros((seq_len, grads.shape[-1]), jnp.float32).at[places].add(grads)


def local(
    hidden_in,
    segments,
    mask_pos,
    target_ids,
    query_emb,
    doc_emb,
    qkv_weight,
    query_bias,
    value_bias,
    out_weight,
    out_bias,
    gain_one,
    shift_one,
    up_weight,
    up_bias,
    down_weight,
    down_bias,
    gain_two,
    shift_two,
    vocab,
):
    f32 = jnp.float32
    bf16 = jnp.bfloat16
    seq_count, _, seq_len, model_width = hidden_in.shape
    pair_count = mask_pos.shape[2]
    mask_count = mask_pos.shape[3]
    head_count = model_width // HEAD_DIM
    score_scale = 1.0 / math.sqrt(HEAD_DIM)
    split_shape = (seq_count, seq_len, head_count, HEAD_DIM)
    tokens = hidden_in.reshape(seq_count, seq_len, model_width)
    segs = segments.reshape(seq_count, seq_len)
    packed = jnp.einsum("nld,de->nle", tokens, qkv_weight, preferred_element_type=f32)
    queries = (packed[..., :model_width] + query_bias).astype(bf16).reshape(split_shape)
    key_rows = packed[..., model_width : 2 * model_width].astype(bf16).reshape(split_shape)
    value_rows = (packed[..., 2 * model_width :] + value_bias).astype(bf16).reshape(split_shape)
    same_seg = (segs[:, :, None] == segs[:, None, :])[:, None]
    raw_scores = jnp.einsum("nlhe,nmhe->nhlm", queries, key_rows, preferred_element_type=f32)

    def attend(scores_in):
        return jax.nn.softmax(jnp.where(same_seg, scores_in * score_scale, -1e30), axis=-1)

    probs, soft_back = jax.vjp(attend, raw_scores)
    probs_low = probs.astype(bf16)
    mixed_heads = jnp.einsum("nhlm,nmhe->nlhe", probs_low, value_rows, preferred_element_type=f32)
    mixed_low = mixed_heads.reshape(seq_count, seq_len, model_width).astype(bf16)
    attended = (
        jnp.einsum("nld,de->nle", mixed_low, out_weight, preferred_element_type=f32) + out_bias
    )
    first_norm, norm_back_one = jax.vjp(
        norm_rows, tokens.astype(f32) + attended, gain_one, shift_one
    )
    first_low = first_norm.astype(bf16)
    inner_act = (
        jnp.einsum("nld,df->nlf", first_low, up_weight, preferred_element_type=f32) + up_bias
    )
    active, gelu_back = jax.vjp(partial(jax.nn.gelu, approximate=False), inner_act)
    active_low = active.astype(bf16)
    second = (
        jnp.einsum("nlf,fd->nld", active_low, down_weight, preferred_element_type=f32) + down_bias
    )
    final_rows, norm_back_two = jax.vjp(norm_rows, first_norm + second, gain_two, shift_two)
    per_seq = pair_count * mask_count
    rows_dev = seq_count * per_seq
    flat_places = mask_pos.reshape(seq_count, per_seq)
    picked = jnp.take_along_axis(final_rows, flat_places[:, :, None], axis=1)
    picked_low = picked.reshape(rows_dev, model_width).astype(bf16)
    logits = lax.dot_general(
        lax.all_gather(picked_low, "batch", axis=0, tiled=True),
        vocab,
        (((1,), (1,)), ((), ())),
        preferred_element_type=f32,
    )
    shard_size = vocab.shape[0]
    vocab_ids = lax.axis_index("batch") * shard_size + lax.iota(jnp.int32, shard_size)
    is_target = target_ids.reshape(-1)[:, None] == vocab_ids[None, :]
    maxima = jnp.max(logits, 1)
    totals = jnp.sum(jnp.exp(logits - maxima[:, None]), 1)
    chosen = jnp.sum(jnp.where(is_target, logits, 0.0), 1)
    maxima, totals, chosen = combined_all((maxima, totals, chosen), "batch", vocab_pair)
    log_total = maxima + jnp.log(totals)
    first_own = lax.axis_index("batch") * rows_dev
    own_logp = lax.dynamic_slice_in_dim(chosen - log_total, first_own, rows_dev)
    reader = jnp.mean(own_logp.reshape(seq_count, pair_count, mask_count), -1)
    gathered_query = lax.all_gather(query_emb, "doc", axis=2, tiled=True)
    doc_rows = doc_emb.reshape(seq_count, pair_count, doc_emb.shape[-1])
    score = jnp.sum(gathered_query * doc_rows, -1)
    joint = score + reader
    unit_terms = jnp.ones_like(score)
    score_top, score_sum = combined_all((score, unit_terms), "doc", lse_pair)
    score_total = score_top + jnp.log(score_sum)
    shifted = joint - score_total
    joint_top, joint_sum = combined_all((shifted, unit_terms), "doc", lse_pair)
    joint_total = joint_top + jnp.log(joint_sum)
    loss = -joint_total
    weight_joint = jnp.exp(shifted - joint_total)
    weight_score = jnp.exp(score - score_total)
    score_grad = weight_score - weight_joint
    grad_query = lax.psum_scatter(
        score_grad[..., None] * doc_rows, "doc", scatter_dimension=2, tiled=True
    )
    row_scale = jnp.broadcast_to(
        (weight_joint / mask_count)[..., None], (seq_count, pair_count, mask_count)
    ).reshape(rows_dev)
    all_scale = lax.all_gather(row_scale, "batch", axis=0, tiled=True)
    vocab_probs = jnp.exp(logits - log_total[:, None])
    logit_grad = (all_scale[:, None] * (vocab_probs - is_target.astype(f32))).astype(bf16)
    picked_grad = lax.psum_scatter(
        jnp.dot(logit_grad, vocab, preferred_element_type=f32).astype(jnp.bfloat16),
        "batch",
        scatter_dimension=0,
        tiled=True,
    ).astype(jnp.float32)
    final_grad = jax.vmap(partial(place_rows, seq_len=seq_len))(
        flat_places, picked_grad.reshape(seq_count, per_seq, model_width)
    )
    sum_grad, grad_gain_two, grad_shift_two = norm_back_two(final_grad)
    grad_down_bias = jnp.sum(sum_grad, (0, 1))
    second_low = sum_grad.astype(bf16)
    grad_down_weight = jnp.einsum("nlf,nld->fd", active_low, second_low, preferred_element_type=f32)
    active_grad = jnp.einsum("nld,fd->nlf", second_low, down_weight, preferred_element_type=f32)
    (inner_grad,) = gelu_back(active_grad)
    grad_up_bias = jnp.sum(inner_grad, (0, 1))
    inner_low = inner_grad.astype(bf16)
    grad_up_weight = jnp.einsum("nld,nlf->df", first_low, inner_low, preferred_element_type=f32)
    first_grad = sum_grad + jnp.einsum(
        "nlf,df->nld", inner_low, up_weight, preferred_element_type=f32
    )
    resid_grad, grad_gain_one, grad_shift_one = norm_back_one(first_grad)
    grad_out_bias = jnp.sum(resid_grad, (0, 1))
    resid_low = resid_grad.astype(bf16)
    grad_out_weight = jnp.einsum("nld,nle->de", mixed_low, resid_low, preferred_element_type=f32)
    mixed_grad = (
        jnp.einsum("nle,de->nld", resid_low, out_weight, preferred_element_type=f32)
        .astype(bf16)
        .reshape(split_shape)
    )
    value_grad = jnp.einsum("nhlm,nlhe->nmhe", probs_low, mixed_grad, preferred_element_type=f32)
    prob_grad = jnp.einsum("nlhe,nmhe->nhlm", mixed_grad, value_rows, preferred_element_type=f32)
    (score_back,) = soft_back(prob_grad)
    score_low = score_back.astype(bf16)
    query_grad = jnp.einsum("nhlm,nmhe->nlhe", score_low, key_rows, preferred_element_type=f32)
    key_grad = jnp.einsum("nhlm,nlhe->nmhe", score_low, queries, preferred_element_type=f32)
    flat_shape = (seq_count, seq_len, model_width)
    query_grad = query_grad.reshape(flat_shape)
    key_grad = key_grad.reshape(flat_shape)
    value_grad = value_grad.reshape(flat_shape)
    grad_query_bias = jnp.sum(query_grad, (0, 1))
    grad_value_bias = jnp.sum(value_grad, (0, 1))
    packed_grad = jnp.concatenate([query_grad, key_grad, value_grad], -1).astype(bf16)
    grad_qkv_weight = jnp.einsum("nld,nle->de", tokens, packed_grad, preferred_element_type=f32)
    input_grad = resid_grad + jnp.einsum(
        "nle,de->nld", packed_grad, qkv_weight, preferred_element_type=f32
    )
    vectors = jnp.concatenate(
        [
            jnp.stack(
                [
                    grad_query_bias,
                    grad_value_bias,
                    grad_out_bias,
                    grad_gain_one,
                    grad_shift_one,
                    grad_down_bias,
                    grad_gain_two,
                    grad_shift_two,
                ]
            ),
            grad_up_bias.reshape(-1, model_width),
        ]
    )
    vectors = jnp.pad(vectors, ((0, -vectors.shape[0] % 16), (0, 0)))
    mats = (grad_down_weight, grad_up_weight, grad_out_weight, grad_qkv_weight)
    down_sum, up_sum, out_sum, qkv_sum, vector_sum = reduce_params(
        [m.astype(bf16) for m in mats], vectors, lax.axis_size("batch"), lax.axis_size("doc")
    )
    nb = lax.axis_size("batch")
    slot = lax.axis_index("batch")

    def share(v):
        return lax.dynamic_slice_in_dim(v, slot * (v.shape[0] // nb), v.shape[0] // nb)

    up_bias_sum = vector_sum[8 : 8 + grad_up_bias.shape[0] // model_width].reshape(-1)
    results = (
        qkv_sum.astype(f32),
        share(vector_sum[0]),
        share(vector_sum[1]),
        out_sum.astype(f32),
        share(vector_sum[2]),
        share(vector_sum[3]),
        share(vector_sum[4]),
        up_sum.astype(f32),
        share(up_bias_sum),
        down_sum.astype(f32),
        share(vector_sum[5]),
        share(vector_sum[6]),
        share(vector_sum[7]),
    )
    block_out = final_rows.astype(bf16).reshape(hidden_in.shape)
    grad_in = input_grad.astype(bf16).reshape(hidden_in.shape)
    return (
        block_out,
        loss,
        grad_in,
        grad_query,
        results[0],
        results[1],
        results[2],
        results[3],
        results[4],
        results[5],
        results[6],
        results[7],
        results[8],
        results[9],
        results[10],
        results[11],
        results[12],
    )


def solution(mesh):
    in_specs = (
        P("batch", "doc", None, None),
        P("batch", "doc", None),
        P("batch", "doc", None, None),
        P(),
        P("batch", None, "doc"),
        P("batch", "doc", None, None),
        P(),
        P(),
        P(),
        P(),
        P(),
        P(),
        P(),
        P(),
        P(),
        P(),
        P(),
        P(),
        P(),
        P("batch", None),
    )
    out_specs = (
        P("batch", "doc", None, None),
        P("batch", None),
        P("batch", "doc", None, None),
        P("batch", None, "doc"),
        P("batch", None),
        P("batch"),
        P("batch"),
        P("batch", None),
        P("batch"),
        P("batch"),
        P("batch"),
        P("batch", None),
        P("batch"),
        P("batch", None),
        P("batch"),
        P("batch"),
        P("batch"),
    )
    return jax.shard_map(local, mesh=mesh, in_specs=in_specs, out_specs=out_specs, check_vma=False)
```

profile of v0, /device:TPU:0, one launch (start us, length us, event | category | flops | bytes accessed | tf_op | source)
XLA Modules:
  0.0 426.0 jit_solution(8762787324111517787)
XLA Ops:
  7.2 0.9 broadcast_in_dim_reshape.8
  8.1 1.3 broadcast_in_dim_reshape.7
  9.4 3.4 convolution_bitcast_fusion
  13.6 1.1 copy.60
  15.0 5.5 %fusion.87 = (f32[12,288]{1,0:T(8,128)S(1)}, f32[12,288,288]{1,2,0:T(8,128)}) fusion(pred[288,288]{0,1:T(8,128)(4,1)S(1)} %broadcast_compare_fusion, bf16[288,12,64]{0,2,1:T(8,128)(2,1)} %bitcast.235, bf16[288,12,64]{0,2,1:T(8,128)(2,1)S(1)} %bitcast.233), kind=kOutput, calls=%fused_computation.186 | convolution fusion | flops 131383584 | bytes 4962816 | tf_op jit(solution)/shard_map/jvp()/sub | solution.py:384
  20.5 2.9 divide_convert_fusion
  23.5 0.7 convolution_convert_fusion.5
  24.2 0.6 copy-done.15
  24.8 1.3 copy-done.27
  26.0 0.7 fusion.88
  27.0 12.6 %multiply_convert_fusion.1 = (bf16[288,3072]{1,0:T(8,128)(2,1)S(1)}, f32[288,3072]{1,0:T(8,128)}, f32[288,3072]{1,0:T(8,128)}) fusion(f32[3072]{0:T(1024)S(1)} %copy-done.29, bf16[768,3072]{1,0:T(8,128)(2,1)} %param.39, f32[288,768]{1,0:T(8,128)S(1)} %get-tuple-element.571, f32[768]{0:T(1024)S(1)} %copy-done.32, f32[768]{0:T(1024)S(1)} %copy-done.24, ...), kind=kOutput, calls=%fused_computation.35 | convolution fusion | flops 1418452992 | bytes 14471424 | tf_op jit(solution)/shard_map/nld,df->nlf/dot_general | solution.py:398
  39.7 1.7 fusion.89
  42.5 1.2 gather_fusion
  43.7 0.9 select_convert_fusion
  44.6 32.7 %all_gather.42 = bf16[256,768]{1,0:T(8,128)(2,1)S(1)} all-gather(bf16[32,768]{1,0:T(8,128)(2,1)S(1)} %select_convert_fusion), channel_id=1, replica_groups=mesh['batch'=8,'doc'=4] {'batch'}, dimensions={0}, use_global_device_ids=true | all-gather | bytes 442368 | tf_op jit(solution)/shard_map/all_gather | solution.py:412
  77.3 1.6 fusion.90
  78.9 20.8 %all-gather.5 = f32[8,1,256]{2,1,0:T(1,128)S(1)} all-gather(f32[1,1,256]{2,1,0:T(1,128)S(1)} %bitcast.259), channel_id=2, replica_groups=mesh['batch'=8,'doc'=4] {'batch'}, dimensions={0}, use_global_device_ids=true | all-gather | bytes 9216 | tf_op jit(solution)/shard_map/all_gather | solution.py:314
  99.7 0.8 eq.40
  100.5 1.6 fusion.23
  102.1 16.3 %all-gather.6 = f32[8,1,256]{2,1,0:T(1,128)S(1)} all-gather(f32[1,1,256]{2,1,0:T(1,128)S(1)} %bitcast.262), channel_id=3, replica_groups=mesh['batch'=8,'doc'=4] {'batch'}, dimensions={0}, use_global_device_ids=true | all-gather | bytes 9216 | tf_op jit(solution)/shard_map/all_gather | solution.py:314
  118.4 18.3 %all-gather.7 = f32[8,1,256]{2,1,0:T(1,128)S(1)} all-gather(f32[1,1,256]{2,1,0:T(1,128)S(1)} %bitcast.261), channel_id=4, replica_groups=mesh['batch'=8,'doc'=4] {'batch'}, dimensions={0}, use_global_device_ids=true | all-gather | bytes 9216 | tf_op jit(solution)/shard_map/all_gather | solution.py:314
  136.7 0.8 copy.63
  137.5 5.2 %all_gather.41 = f32[1,4,128]{1,0,2:T(1,128)S(1)} all-gather(f32[1,4,32]{1,0,2:T(1,128)S(1)} %copy.63), channel_id=1, replica_groups=mesh['batch'=8,'doc'=4] {'doc'}, dimensions={2}, use_global_device_ids=true | all-gather | bytes 2560 | tf_op jit(solution)/shard_map/all_gather | solution.py:428
  142.7 0.8 copy.64
  143.6 1.2 dynamic-slice.8
  145.8 7.0 %all-reduce.1 = f32[16]{0:T(128)S(1)} all-reduce(f32[16]{0:T(128)S(1)} %dynamic-update-slice), channel_id=5, replica_groups=mesh['batch'=8,'doc'=4] {'doc'}, use_global_device_ids=true, to_apply=%add.1 | all-reduce | flops 16 | bytes 128
  152.9 0.6 while.55
  153.9 5.0 %all-gather.8 = f32[4,1,4]{2,1,0:T(1,128)S(1)} all-gather(f32[1,1,4]{2,1,0:T(1,128)S(1)} %bitcast.260), channel_id=6, replica_groups=mesh['batch'=8,'doc'=4] {'doc'}, dimensions={0}, use_global_device_ids=true | all-gather | bytes 80 | tf_op jit(solution)/shard_map/all_gather | solution.py:314
  159.1 0.5 fusion.65
  159.6 0.7 broadcast_multiply_fusion
  160.5 0.6 dynamic-slice.9
  162.0 17.1 %all-reduce.2 = f32[256]{0:T(256)S(1)} all-reduce(f32[256]{0:T(256)S(1)} %dynamic-update-slice.1), channel_id=1, replica_groups=mesh['batch'=8,'doc'=4] {'batch'}, use_global_device_ids=true, to_apply=%add.2 | all-reduce | flops 256 | bytes 2048
  179.1 2.7 convolution_convert_fusion.7
  182.0 1.0 fusion.123
  183.0 1.4 copy.76
  184.4 57.5 %reduce-scatter.5.cloned.1.call-done = bf16[32,768]{1,0:T(8,128)(2,1)} async-done(((bf16[256,768]{1,0:T(8,128)(2,1)}), bf16[32,768]{1,0:T(8,128)(2,1)}) %reduce-scatter.5.cloned.1.call-update) | async-done | bytes 49168 | tf_op jit(solution)/shard_map/reduce_scatter | solution.py:451
  241.8 1.3 scatter_custom_fusion
  243.9 1.5 copy-done.39
  245.5 7.2 %fusion.91 = (f32[3072]{0:T(1024)S(1)}, bf16[288,3072]{1,0:T(8,128)(2,1)S(1)}) fusion(f32[288,3072]{1,0:T(8,128)S(1)} %copy-done.39, f32[288,3072]{1,0:T(8,128)} %get-tuple-element.572, bf16[3072,768]{1,0:T(8,128)(2,1)} %param.41, f32[1,288,768]{2,1,0:T(8,128)S(1)} %get-tuple-element.544, f32[288]{0:T(512)S(1)} %negate_multiply_fusion.2), kind=kOutput, calls=%fused_computation.190 | convolution fusion | flops 1372664832 | bytes 14464128 | tf_op jit(solution)/shard_map/nld,fd->nlf/dot_general | solution.py:464
  252.7 1.9 fusion.30
  255.1 0.6 convolution_convert_fusion.6
  256.0 3.0 fusion.84
  259.0 3.5 multiply_reduce_fusion
  262.7 1.1 multiply_convert_fusion
  263.8 1.0 convolution_convert_fusion.4
  264.9 0.7 fusion.85
  265.8 4.4 %convolution_convert_fusion.2 = bf16[3072,768]{1,0:T(8,128)(2,1)} fusion(bf16[288,3072]{1,0:T(8,128)(2,1)S(1)} %copy-done.36, f32[1,288,768]{2,1,0:T(8,128)S(1)} %copy-done.8, f32[288]{0:T(512)S(1)} %negate_multiply_fusion.2), kind=kOutput, calls=%fused_computation.29 | convolution fusion | flops 1361756160 | bytes 7373952 | tf_op jit(solution)/shard_map/nlf,nld->fd/dot_general | solution.py:463
  270.2 5.0 %convolution_convert_fusion.1 = bf16[768,3072]{1,0:T(8,128)(2,1)} fusion(bf16[288,3072]{1,0:T(8,128)(2,1)S(1)} %copy-done.38, f32[288,768]{1,0:T(8,128)S(1)} %copy-done.6, f32[768]{0:T(1024)S(1)} %copy-done.33, f32[768]{0:T(1024)S(1)} %copy-done.24, f32[288]{0:T(512)S(1)} %fusion.50, f32[288]{0:T(512)S(1)} %broadcast_multiply_fusion.2), kind=kOutput, calls=%fused_computation.28 | convolution fusion | flops 1362419712 | bytes 7381248 | tf_op jit(solution)/shard_map/nld,nlf->df/dot_general | solution.py:468
  275.2 1.9 convolution_convert_fusion.3
  277.1 2.5 fusion.22
  279.6 3.8 convolution_convert_fusion
  284.1 0.6 pad.4.refs_4_
  284.7 122.3 %shard_map.323 = (bf16[384,768]{1,0:T(8,128)(2,1)}, bf16[96,3072]{1,0:T(8,128)(2,1)}, bf16[96,768]{1,0:T(8,128)(2,1)}, bf16[96,2304]{1,0:T(8,128)(2,1)}, f32[16,768]{1,0:T(8,128)}) custom-call(bf16[2,2,2,384,768]{4,3,2,1,0:T(8,128)(2,1)} %bitcast.230, bf16[2,2,2,96,3072]{4,3,2,1,0:T(8,128)(2,1)} %bitcast.231, bf16[2,2,2,96,768]{4,3,2,1,0:T(8,128)(2,1)} %bitcast.229, ...), custom_call_target="tpu_custom_call" | custom-call | tf_op jit(solution)/shard_map/pallas_call | solution.py:300
  407.0 1.1 fusion.86
  408.1 0.7 slice.67
  408.8 2.0 convert_element_type.140
  410.8 1.6 convert_element_type.141
  412.4 2.2 convert_element_type.142
  414.6 1.1 convert_element_type.143
  415.7 0.6 fusion.53
  416.3 0.6 fusion.55
  416.9 0.6 fusion.57
  417.5 0.7 dynamic_slice.117
  418.1 0.6 fusion.59
  (201 shorter events, 6.9 us)
Async XLA Ops:
  7.2 70.2 %copy-start = (bf16[1024,768]{1,0:T(8,128)(2,1)S(1)}, bf16[1024,768]{1,0:T(8,128)(2,1)}, u32[]{:S(2)}) copy-start(bf16[1024,768]{1,0:T(8,128)(2,1)} %param.45) | copy-start | bytes 4718596
  7.2 175.8 %reduce-scatter.7.cloned.1.call-start = ((), (), s32[]{:S(2)}) async-start(), calls=%async_computation.3 | async-start | bytes 81920
  9.4 3.4 copy-start.22
  9.4 3.5 copy-start.23
  12.8 0.7 copy-start.25
  13.6 6.9 %copy-start.17 = (pred[288,288]{0,1:T(8,128)(4,1)}, pred[288,288]{0,1:T(8,128)(4,1)S(1)}, u32[]{:S(2)}) copy-start(pred[288,288]{0,1:T(8,128)(4,1)S(1)} %broadcast_compare_fusion) | copy-start | bytes 248836
  15.0 5.5 %copy-start.9 = (bf16[1,288,768]{1,2,0:T(8,128)(2,1)}, bf16[1,288,768]{1,2,0:T(8,128)(2,1)S(1)}, u32[]{:S(2)}) copy-start(bf16[1,288,768]{1,2,0:T(8,128)(2,1)S(1)} %copy.61) | copy-start | bytes 1327108
  23.4 3.5 copy-start.2
  23.4 1.3 copy-start.15
  23.5 2.6 copy-start.27
  23.5 2.6 copy-start.30
  23.5 3.5 copy-start.24
  23.5 3.5 copy-start.29
  23.5 3.5 copy-start.32
  24.2 15.4 %copy-start.12 = (bf16[12,64,288]{2,1,0:T(8,128)(2,1)}, bf16[12,64,288]{2,1,0:T(8,128)(2,1)S(1)}, u32[]{:S(2)}) copy-start(bf16[12,64,288]{2,1,0:T(8,128)(2,1)S(1)} %convolution_convert_fusion.5) | copy-start | bytes 1327108
  26.0 13.6 %slice-start.2 = ((s8[4718592]{0:T(1024)(128)(4,1)}), s8[524288]{0:T(1024)(128)(4,1)S(1)}, s32[]{:S(2)}) async-start(s8[4718592]{0:T(1024)(128)(4,1)} %bitcast.263), calls=%async_computation.6 | async-start | bytes 1048576
  26.7 12.9 %copy-start.4 = (f32[288,768]{1,0:T(8,128)}, f32[288,768]{1,0:T(8,128)S(1)}, u32[]{:S(2)}) copy-start(f32[288,768]{1,0:T(8,128)S(1)} %get-tuple-element.571) | copy-start | bytes 2654212
  27.0 12.6 %slice-start.3 = ((s8[4718592]{0:T(1024)(128)(4,1)}), s8[4194304]{0:T(1024)(128)(4,1)S(1)}, s32[]{:S(2)}) async-start(s8[4718592]{0:T(1024)(128)(4,1)} %bitcast.263), calls=%async_computation.7 | async-start | bytes 8388608
  27.0 12.6 %copy-start.31 = (f32[768]{0:T(1024)S(1)}, f32[768]{0:T(1024)}, u32[]{:S(2)}) copy-start(f32[768]{0:T(1024)} %param.42) | copy-start | bytes 9220
  39.6 1.8 copy-start.35
  39.7 2.0 copy-start.26
  39.7 2.5 copy-start.19
  39.7 2.5 copy-start.21
  43.7 116.8 %copy-start.34 = (u32[32]{0:T(128)S(1)}, u32[32]{0:T(128)}, u32[]{:S(2)}) copy-start(u32[32]{0:T(128)} %constant.263) | copy-start | bytes 388
  78.9 102.9 %copy-start.20 = (s32[1,1,4,8]{3,2,1,0:T(4,128)S(1)}, s32[1,1,4,8]{3,2,1,0:T(4,128)}, u32[]{:S(2)}) copy-start(s32[1,1,4,8]{3,2,1,0:T(4,128)} %param.28) | copy-start | bytes 388
  160.3 81.5 %reduce-scatter.5.cloned.1.call-start = ((), (), s32[]{:S(2)}) async-start(), calls=%async_computation.2 | async-start | bytes 442368 | tf_op jit(solution)/shard_map/reduce_scatter | solution.py:451
  243.1 2.3 copy-start.39
  243.5 9.2 %slice-start.4 = ((s8[4718592]{0:T(1024)(128)(4,1)}), s8[4194304]{0:T(1024)(128)(4,1)S(1)}, s32[]{:S(2)}) async-start(s8[4718592]{0:T(1024)(128)(4,1)} %bitcast.265), calls=%async_computation.8 | async-start | bytes 8388608
  243.9 8.8 %copy-start.7 = (f32[1,288,768]{2,1,0:T(8,128)}, f32[1,288,768]{2,1,0:T(8,128)S(1)}, u32[]{:S(2)}) copy-start(f32[1,288,768]{2,1,0:T(8,128)S(1)} %get-tuple-element.544) | copy-start | bytes 2654212
  245.5 7.2 %copy-start.5 = (f32[288,768]{1,0:T(8,128)S(1)}, f32[288,768]{1,0:T(8,128)}, u32[]{:S(2)}) copy-start(f32[288,768]{1,0:T(8,128)} %copy-done.4) | copy-start | bytes 2654212
  245.5 7.3 %slice-start.5 = ((s8[4718592]{0:T(1024)(128)(4,1)}), s8[524288]{0:T(1024)(128)(4,1)S(1)}, s32[]{:S(2)}) async-start(s8[4718592]{0:T(1024)(128)(4,1)} %bitcast.265), calls=%async_computation.9 | async-start | bytes 1048576
  252.7 2.0 copy-start.37
  252.7 2.4 copy-start.28
  256.0 6.6 %slice-start = ((s8[5308416]{0:T(1024)(128)(4,1)}), s8[4194304]{0:T(1024)(128)(4,1)S(1)}, s32[]{:S(2)}) async-start(s8[5308416]{0:T(1024)(128)(4,1)} %bitcast.223), calls=%async_computation.4 | async-start | bytes 8388608
  259.0 3.6 slice-start.1
  259.0 3.6 copy-start.18
  262.6 1.2 copy-start.11
  263.8 1.1 copy-start.10
  263.8 1.8 copy-start.8
  263.8 1.9 copy-start.36
  265.7 4.4 %copy-start.6 = (f32[288,768]{1,0:T(8,128)S(1)}, f32[288,768]{1,0:T(8,128)}, u32[]{:S(2)}) copy-start(f32[288,768]{1,0:T(8,128)} %copy-done.4) | copy-start | bytes 2654212
  265.7 4.4 %copy-start.33 = (f32[768]{0:T(1024)S(1)}, f32[768]{0:T(1024)}, u32[]{:S(2)}) copy-start(f32[768]{0:T(1024)} %param.38) | copy-start | bytes 9220
  265.7 4.4 %copy-start.38 = (bf16[288,3072]{1,0:T(8,128)(2,1)S(1)}, bf16[288,3072]{1,0:T(8,128)(2,1)}, u32[]{:S(2)}) copy-start(bf16[288,3072]{1,0:T(8,128)(2,1)} %copy-done.37) | copy-start | bytes 5308420
  270.1 5.0 %copy-start.13 = (bf16[12,64,288]{2,1,0:T(8,128)(2,1)S(1)}, bf16[12,64,288]{2,1,0:T(8,128)(2,1)}, u32[]{:S(2)}) copy-start(bf16[12,64,288]{2,1,0:T(8,128)(2,1)} %copy-done.12) | copy-start | bytes 1327108
  270.1 6.9 %copy-start.3 = (bf16[768,2304]{1,0:T(8,128)(2,1)S(1)}, bf16[768,2304]{1,0:T(8,128)(2,1)}, u32[]{:S(2)}) copy-start(bf16[768,2304]{1,0:T(8,128)(2,1)} %param.32) | copy-start | bytes 10616836
  277.1 2.5 copy-start.16
  284.7 134.0 %copy-start.1 = (bf16[1024,768]{1,0:T(8,128)(2,1)S(1)}, bf16[1024,768]{1,0:T(8,128)(2,1)}, u32[]{:S(2)}) copy-start(bf16[1024,768]{1,0:T(8,128)(2,1)} %param.45) | copy-start | bytes 4718596
  407.0 7.6 %copy-start.14 = (bf16[384,768]{1,0:T(8,128)(2,1)S(1)}, bf16[384,768]{1,0:T(8,128)(2,1)}, u32[]{:S(2)}) copy-start(bf16[384,768]{1,0:T(8,128)(2,1)} %get-tuple-element.455) | copy-start | bytes 1769476
Sparse Core Ops, SparseCore 0:
  160.4 15.7 reduce-scatter.6
  182.0 59.8 reduce-scatter.4
where the time goes:
time: 432 us; the launch traced here: 426 us
  blocking collectives  122 us (28%)
  Pallas kernels  122 us (28%)
  matrix products  64.4 us (15%)
  waiting for transfers between devices  57.5 us (13%)
  local copies, waits for them, and re-layouts  21.6 us (5%)
  other arithmetic  20.7 us (5%)
  between operations  16.6 us (4%)
    pallas_call x1, Pallas kernels, reduce_params(): pl.pallas_call(partial(reduce_kernel, pieces, halves, order, len(mats)),...  122 us
    all_gather x4, blocking collectives, combined_all(): everything = jax.tree.map(lambda part: lax.all_gather(part, axis), x)  60.3 us
    reduce_scatter x1, waiting for transfers between devices, local(): lax.psum_scatter(jnp.dot(logit_grad, vocab, preferred_element_type=f32).a...  57.5 us
    all_gather x1, blocking collectives, local(): lax.all_gather(picked_low, 'batch', axis=0, tiled=True)  32.7 us
    unnamed x2, blocking collectives  24.2 us
    dot_general x1, matrix products, local(): jnp.einsum('nld,df->nlf', first_low, up_weight, preferred_element_type=f32)  12.6 us
    unnamed x104, local copies, waits for them, and re-layouts  9.06 us
  transfers between devices with their start and end apart: 2, of which 1 were waited for; matrix products, arithmetic and copies ran while one was open for 1% of the time, Pallas kernels for 0%

commit v1 on v0

--- a/solution.py
+++ b/solution.py
@@ -308,6 +308,737 @@
             collective_id=0, has_side_effects=True, vmem_limit_bytes=VMEM_BYTES
         ),
     )(*[m.reshape((2,) * len(batch) + (m.shape[0] // nb, m.shape[1])) for m in mats], vectors)
+
+
+F32, BF16 = jnp.float32, jnp.bfloat16
+NT = (((1,), (1,)), ((), ()))
+TN = (((0,), (0,)), ((), ()))
+EPS = 1e-06
+
+
+def mm(a, b):
+    return jnp.dot(a, b, preferred_element_type=F32)
+
+
+def mm_nt(a, b):
+    return lax.dot_general(a, b, NT, preferred_element_type=F32)
+
+
+def mm_tn(a, b):
+    return lax.dot_general(a, b, TN, preferred_element_type=F32)
+
+
+def mm_exact(a, b, dims=(((1,), (0,)), ((), ()))):
+    return lax.dot_general(a, b, dims, preferred_element_type=F32, precision=lax.Precision.HIGHEST)
+
+
+def iota(shape, axis):
+    return lax.broadcasted_iota(jnp.int32, shape, axis)
+
+
+def normed(z):
+    centred = z - jnp.mean(z, -1, keepdims=True)
+    rstd = lax.rsqrt(jnp.mean(centred * centred, -1, keepdims=True) + EPS)
+    return centred * rstd, rstd
+
+
+def norm_back(grad, hat, rstd, gain):
+    g = grad * gain
+    inner = g - jnp.mean(g, -1, keepdims=True) - hat * jnp.mean(g * hat, -1, keepdims=True)
+    return rstd * inner
+
+
+def gelu(x):
+    return 0.5 * x * (1.0 + lax.erf(x * math.sqrt(0.5)))
+
+
+def gelu_slope(x):
+    density = jnp.exp(-0.5 * x * x) * (1.0 / math.sqrt(2.0 * math.pi))
+    return 0.5 * (1.0 + lax.erf(x * math.sqrt(0.5))) + x * density
+
+
+def column_of(row_block):
+    n, m = row_block.shape
+    diag = iota((m, m), 0) == iota((m, m), 1)
+    cols = [
+        jnp.sum(jnp.where(diag, jnp.broadcast_to(row_block[i : i + 1, :], (m, m)), 0), 1, keepdims=True)
+        for i in range(n)
+    ]
+    return jnp.concatenate(cols, 0)
+
+
+class Net:
+    def __init__(self, send, recv):
+        self.send, self.recv, self.used, self.open = send, recv, 0, []
+
+    def take(self, n=1):
+        self.used += n
+        return self.used - n
+
+    def copy(self, src, dst, peer, send_at, recv_at):
+        return pltpu.make_async_remote_copy(
+            src_ref=src,
+            dst_ref=dst,
+            send_sem=self.send.at[send_at],
+            recv_sem=self.recv.at[recv_at],
+            device_id=peer,
+            device_id_type=MESH,
+        )
+
+    def put(self, src, dst, peer, send_at, recv_at):
+        copy = self.copy(src, dst, peer, send_at, recv_at)
+        copy.start()
+        self.open.append((None, copy))
+        return copy
+
+    def put_if(self, cond, src, dst, peer, send_at, recv_at):
+        copy = self.copy(src, dst, peer, send_at, recv_at)
+        pl.when(cond)(copy.start)
+        self.open.append((cond, copy))
+        return copy
+
+    def drain(self):
+        for cond, copy in self.open:
+            if cond is None:
+                copy.wait_send()
+            else:
+                pl.when(cond)(copy.wait_send)
+        self.open = []
+
+
+class Trip:
+    def __init__(self, tile, lead, halve, both, spread, twin):
+        self.tile, self.lead, self.halve, self.both = tile, lead, halve, both
+        self.steps = [("halve", k) for k in halve] + [("both", k) for k in both]
+        self.sums = len(self.steps)
+        self.steps += [("spread", k) for k in spread] + ([("twin", ("doc", 0))] if twin else [])
+        self.spread, self.twin = spread, twin
+
+    def buffers(self):
+        shapes = [(2,) * len(self.lead) + self.tile]
+        shapes += [(2,) * (len(self.lead) - i - 1) + self.tile for i in range(len(self.halve))]
+        shapes += [self.tile] * len(self.both)
+        return shapes + [(2,) * (self.twin + len(self.spread)) + self.tile]
+
+    def bytes(self, i):
+        kind, key = self.steps[i]
+        unit = 2 * math.prod(self.tile)
+        if kind == "halve":
+            return unit * 2 ** (len(self.lead) - i - 1)
+        return unit * (2 ** len(self.spread) if kind == "twin" else 1)
+
+
+class TripRun:
+    def __init__(self, trip, bufs, net, spot):
+        self.t, self.bufs, self.net, self.spot = trip, bufs, net, spot
+        self.base = net.take(len(trip.steps))
+        self.live, self.copies = {}, []
+
+    @property
+    def final(self):
+        return self.bufs[-1]
+
+    def at(self, fixed):
+        return tuple(fixed.get(key, slice(None)) for key in self.t.lead)
+
+    def place(self):
+        return ((self.spot.mine(("doc", 0)),) if self.t.twin else ()) + tuple(
+            self.spot.mine(k) for k in self.t.spread
+        )
+
+    def start(self, step):
+        kind, key = self.t.steps[step]
+        if kind == "halve":
+            src = self.bufs[0].at[self.at({**self.live, key: 1 - self.spot.mine(key)})]
+            dst = self.bufs[1 + step]
+        elif kind == "both":
+            src, dst = self.bufs[0].at[self.at(self.live)], self.bufs[1 + step]
+        elif kind == "spread":
+            src = dst = self.final.at[self.place()]
+        else:
+            src = dst = self.final.at[self.spot.mine(key)]
+        at = self.base + step
+        copy = self.net.copy(src, dst, self.spot.peer(key), at, at)
+        copy.start()
+        self.copies.append(copy)
+
+    def finish(self, step):
+        kind, key = self.t.steps[step]
+        copy = self.copies[step]
+        copy.wait_recv()
+        if kind == "both":
+            copy.wait_send()
+        else:
+            self.net.open.append((None, copy))
+        if step < self.t.sums:
+            if kind == "halve":
+                self.live[key] = self.spot.mine(key)
+            got = self.bufs[1 + step]
+            free = [k for k in self.t.lead if k not in self.live]
+            for pick in itertools.product(range(2), repeat=len(free)):
+                at = self.at({**self.live, **dict(zip(free, pick))})
+                total = self.bufs[0][at] + got[pick]
+                if step + 1 == self.t.sums:
+                    self.final[self.place()] = total
+                else:
+                    self.bufs[0][at] = total
+
+
+def layer_trips(share):
+    y, z0, z1, x = ("batch", 0), ("batch", 1), ("batch", 2), ("doc", 1)
+    block = [Trip((share, 384), [z1, y], [y, z1], [], [x], True) for _ in range(5)]
+    wide = [Trip((share, 128), [x, z1, z0, y], [x, y, z0, z1], [], [x], True) for _ in range(3)]
+    small = Trip((16, 768), [], [], [y, z0, z1, x, ("doc", 0)], [], False)
+    return block + wide + [small]
+
+
+def layer_kernel(trips, *refs):
+    (
+        hidden, segs, places, targets, query, doc_rows,
+        bias_q, bias_v, bias_o, gain1, shift1, bias_up, bias_down, gain2, shift2,
+        qkv_hbm, out_hbm, up_hbm, down_hbm, vocab_hbm,
+        block_out, loss_out, grad_in, grad_query, mats_out, wide_out, vec_out,
+        wqkv, wout, wup, wdown, wvoc,
+        qb, kb, vb, mixed, first_norm, first_low, acc,
+        x2, x2t, kvb, kv2,
+        picks, tsend, trecv, usend, urecv, ssend, srecv, logits,
+        qexp, probs, probs_low,
+        hints, hints_in, joint, joint_in,
+        a_send, a_mixed, a1, a2, at, second_b, inner_b, rest_b, g1, g2,
+        vecs,
+        load_sem, send, recv, *trip_bufs,
+    ) = refs
+    spot = Spot()
+    batch, doc = spot.at["batch"], spot.at["doc"]
+    nb, nd = lax.axis_size("batch"), lax.axis_size("doc")
+    core, x = spot.mine(("doc", 0)), spot.mine(("doc", 1))
+    z0 = spot.mine(("batch", 1))
+    rows, width = hidden.shape
+    pairs, slots = places.shape
+    n_pick = pairs * slots
+    heads = width // HEAD_DIM
+    share = width // nb
+    net = Net(send, recv)
+
+    loads = [
+        pltpu.make_async_copy(qkv_hbm.at[:, pl.ds(width, 2 * width)], wqkv.at[:, pl.ds(width, 2 * width)], load_sem.at[0]),
+        pltpu.make_async_copy(qkv_hbm.at[:, pl.ds(0, width)], wqkv.at[:, pl.ds(0, width)], load_sem.at[1]),
+        pltpu.make_async_copy(out_hbm, wout, load_sem.at[2]),
+        pltpu.make_async_copy(up_hbm, wup, load_sem.at[3]),
+        pltpu.make_async_copy(down_hbm, wdown, load_sem.at[4]),
+        pltpu.make_async_copy(vocab_hbm, wvoc, load_sem.at[5]),
+    ]
+    for load in loads:
+        load.start()
+
+    batch_peers = [(lax.rem(batch + j, nb), doc) for j in range(1, nb)]
+    doc_peers = [(batch, lax.rem(doc + j, nd)) for j in range(1, nd)]
+    sides = [(dx, dz) for dz in range(2) for dx in range(2)]
+
+    def side_peer(dx, dz, to_core):
+        tx = lax.rem(x + dx, 2)
+        tz = lax.rem(z0 + dz, 2)
+        return (batch + 2 * (tz - z0), 2 * tx + to_core), tx, tz
+
+    far = [side_peer(1, 1, core)[0], side_peer(1, 1, 1 - core)[0], side_peer(0, 1, 1 - core)[0]]
+    everyone = batch_peers + doc_peers + far
+    barrier = pltpu.get_barrier_semaphore()
+    for peer in everyone:
+        pl.semaphore_signal(barrier, inc=1, device_id=peer, device_id_type=MESH)
+    pl.semaphore_wait(barrier, len(everyone))
+
+    own_part = query.shape[1]
+    spread_lanes = (iota((own_part, own_part * nd), 0) + own_part * doc == iota((own_part, own_part * nd), 1)).astype(F32)
+    hints[0:pairs, :] = mm_exact(query[...], spread_lanes)
+    hints[8 : 8 + pairs, :] = doc_rows[...]
+    hints_in[doc, 0:pairs, :] = hints[0:pairs, :]
+    hints_in[doc, 8 : 8 + pairs, :] = hints[8 : 8 + pairs, :]
+    hint_at = net.take(nd)
+    hint_copies = [
+        net.put(hints, hints_in.at[doc], peer, hint_at + j + 1, hint_at + j + 1) for j, peer in enumerate(doc_peers)
+    ]
+    twin = spot.peer(("doc", 0))
+    x2_at = net.take()
+    x2_copy = net.put(hidden, x2.at[pl.ds(rows, rows)], twin, x2_at, x2_at)
+    x2[0:rows, :] = hidden[...]
+
+    place_col = column_of(places[...])
+    pick_bool = iota((n_pick, rows), 1) == place_col
+    pick = pick_bool.astype(BF16)
+    pick_f32 = pick_bool.astype(F32)
+    tokens = hidden[...]
+    loads[0].wait()
+    kb[...] = mm(tokens, wqkv[:, width : 2 * width]).astype(BF16)
+    vb[...] = (mm(tokens, wqkv[:, 2 * width :]) + bias_v[...]).astype(BF16)
+    tokens_p = mm(pick, tokens).astype(BF16)
+    loads[1].wait()
+    query_p = (mm(tokens_p, wqkv[:, 0:width]) + bias_q[...]).astype(BF16)
+
+    tall = heads * n_pick
+    own_head = iota((tall, width), 0) // n_pick == iota((tall, width), 1) // HEAD_DIM
+
+    def expand(v):
+        return jnp.where(own_head, jnp.concatenate([v] * heads, 0), jnp.zeros((), v.dtype))
+
+    def fold(v):
+        return jnp.sum(jnp.where(own_head, v, 0.0).reshape(heads, n_pick, width), 0)
+
+    seg_row = segs[...]
+    seg_pick = jnp.sum(jnp.where(pick_bool, jnp.broadcast_to(seg_row, (n_pick, rows)), 0), 1, keepdims=True)
+    same_pick = seg_pick == seg_row
+    scale = 1.0 / math.sqrt(HEAD_DIM)
+    qexp[...] = expand(query_p)
+    scores = mm_nt(qexp[...], kb[...]) * scale
+    same_tall = jnp.concatenate([same_pick.astype(F32)] * heads, 0) > 0.5
+    scores = jnp.where(same_tall, scores, -1e30)
+    weights = jnp.exp(scores - jnp.max(scores, -1, keepdims=True))
+    weights = weights / jnp.sum(weights, -1, keepdims=True)
+    probs[...] = weights
+    probs_low[...] = weights.astype(BF16)
+    mixed_p = fold(mm(probs_low[...], vb[...])).astype(BF16)
+    loads[2].wait()
+    attended = mm(mixed_p, wout[...]) + bias_o[...]
+    hat1, rstd1 = normed(tokens_p.astype(F32) + attended)
+    first_p = hat1 * gain1[...] + shift1[...]
+    first_low_p = first_p.astype(BF16)
+    loads[3].wait()
+    inner_p = mm(first_low_p, wup[...]) + bias_up[...]
+    active_p = gelu(inner_p).astype(BF16)
+    loads[4].wait()
+    second_p = mm(active_p, wdown[...]) + bias_down[...]
+    hat2, rstd2 = normed(first_p + second_p)
+    picks[batch] = (hat2 * gain2[...] + shift2[...]).astype(BF16)
+    pick_at = net.take(nb)
+    pick_copies = [
+        net.put(picks.at[batch], picks.at[batch], peer, pick_at + j + 1, pick_at + j + 1)
+        for j, peer in enumerate(batch_peers)
+    ]
+
+    ff = wup.shape[1]
+    for k in range(2):
+        for half in range(2):
+            start = (2 * half + k) * 2 * (ff // nb)
+            a_send[k, :, half * width : (half + 1) * width] = active_p[:, start : start + width]
+    a_send[2, :, 0:width] = first_low_p
+    a_send[2, :, width : 2 * width] = tokens_p
+    a_mixed[...] = mixed_p
+    slot = 4 * z0 + doc
+    a1_at, a2_at = net.take(8), net.take(8)
+    a1[slot] = a_send[(1 - core) * z0 + 2 * core]
+    a2[slot] = a_mixed[...]
+
+    def send_left(k):
+        dx, dz = sides[k]
+        for other in range(2):
+            if k == 0 and other == 0:
+                continue
+            to_core = core if other == 0 else 1 - core
+            peer, tx, tz = side_peer(dx, dz, to_core)
+            part = a_send.at[(1 - to_core) * tz + 2 * to_core]
+            net.put(part, a1.at[slot], peer, a1_at + 2 * k + other, a1_at + 2 * k + other)
+            net.put(a_mixed, a2.at[slot], peer, a2_at + 2 * k + other, a2_at + 2 * k + other)
+
+    def wait_left():
+        for k in range(4):
+            for other in range(2):
+                if k or other:
+                    i = 2 * k + other
+                    net.copy(a_send.at[0], a1.at[slot], twin, a1_at + i, a1_at + i).wait_recv()
+                    net.copy(a_mixed, a2.at[slot], twin, a2_at + i, a2_at + i).wait_recv()
+
+    send_left(0)
+    send_left(1)
+
+    loads[5].wait()
+    entries = wvoc.shape[0]
+    target_col = jnp.concatenate([column_of(targets[j]) for j in range(nb)], 0) - batch * entries
+    all_rows = nb * n_pick
+    is_target = iota((all_rows, entries), 1) == target_col
+    tsend[...] = mm(is_target.astype(BF16), wvoc[...]).astype(BF16).reshape(nb, n_pick, width)
+    trecv[batch] = tsend[batch]
+    t_at = net.take(nb)
+    t_copies = [
+        net.put(tsend.at[peer[0]], trecv.at[batch], peer, t_at + j + 1, t_at + j + 1)
+        for j, peer in enumerate(batch_peers)
+    ]
+
+    seg_col = jnp.sum(
+        jnp.where(iota((rows, rows), 0) == iota((rows, rows), 1), jnp.broadcast_to(seg_row, (rows, rows)), 0),
+        1,
+        keepdims=True,
+    )
+    qb[...] = (mm(tokens, wqkv[:, 0:width]) + bias_q[...]).astype(BF16)
+
+    def attend(i):
+        lanes = pl.ds(pl.multiple_of(i * 128, 128), 128)
+        q_s, k_s, v_s = qb[:, lanes], kb[:, lanes], vb[:, lanes]
+        low = iota((rows, 128), 1) < HEAD_DIM
+        same = seg_col == seg_row
+        parts = []
+        for side in (low, ~low):
+            s = mm_nt(jnp.where(side, q_s, jnp.zeros((), BF16)), k_s) * scale
+            s = jnp.where(same, s, -1e30)
+            e = jnp.exp(s - jnp.max(s, -1, keepdims=True))
+            p = (e / jnp.sum(e, -1, keepdims=True)).astype(BF16)
+            parts.append(mm(p, v_s))
+        mixed[:, lanes] = jnp.where(low, parts[0], parts[1]).astype(BF16)
+
+    pl.loop(0, width // 128)(attend)
+
+    for copy in pick_copies:
+        copy.wait_recv()
+    logits[...] = mm_nt(picks[...].reshape(all_rows, width), wvoc[...])
+    lg = logits[...]
+    top = jnp.max(lg, 1, keepdims=True)
+    chosen = jnp.sum(jnp.where(is_target, lg, 0.0), 1, keepdims=True)
+    others = jnp.where(is_target, 0.0, jnp.exp(lg - top))
+    total = jnp.sum(others, 1, keepdims=True)
+    lane = iota((all_rows, 128), 1)
+    stats = jnp.where(lane == 0, top, jnp.where(lane == 1, total, chosen))
+    ssend[...] = stats.reshape(nb, n_pick, 128)
+    usend[...] = mm(others.astype(BF16), wvoc[...]).astype(BF16).reshape(nb, n_pick, width)
+    srecv[batch] = ssend[batch]
+    urecv[batch] = usend[batch]
+    s_at, u_at = net.take(nb), net.take(nb)
+    s_copies, u_copies = [], []
+    for j, peer in enumerate(batch_peers):
+        s_copies.append(net.put(ssend.at[peer[0]], srecv.at[batch], peer, s_at + j + 1, s_at + j + 1))
+        u_copies.append(net.put(usend.at[peer[0]], urecv.at[batch], peer, u_at + j + 1, u_at + j + 1))
+
+    tokens = hidden[...]
+    hat, _ = normed(tokens.astype(F32) + mm(mixed[...], wout[...]) + bias_o[...])
+    first_norm[...] = hat * gain1[...] + shift1[...]
+    first_low[...] = first_norm[...].astype(BF16)
+    acc[...] = first_norm[...] + bias_down[...]
+    chunk = 512
+
+    def feed(i):
+        cols = pl.ds(pl.multiple_of(i * chunk, chunk), chunk)
+        hid = mm(first_low[...], wup[:, cols]) + bias_up[:, cols]
+        acc[...] += mm(gelu(hid).astype(BF16), wdown[cols, :])
+
+    pl.loop(0, ff // chunk)(feed)
+    hat, _ = normed(acc[...])
+    block_out[...] = (hat * gain2[...] + shift2[...]).astype(BF16)
+    x2_copy.wait_recv()
+    x2t[...] = x2[...].T
+
+    for group in (s_copies, t_copies, u_copies):
+        for copy in group:
+            copy.wait_recv()
+    send_left(2)
+    send_left(3)
+    tops = [srecv[j][:, 0:1] for j in range(nb)]
+    peak = tops[0]
+    for t in tops[1:]:
+        peak = jnp.maximum(peak, t)
+    rest = jnp.zeros_like(peak)
+    chosen = jnp.zeros_like(peak)
+    mixture = jnp.zeros((n_pick, width), F32)
+    target_rows = jnp.zeros((n_pick, width), F32)
+    for j in range(nb):
+        factor = jnp.exp(tops[j] - peak)
+        rest += factor * srecv[j][:, 1:2]
+        chosen += srecv[j][:, 2:3]
+        mixture += factor * urecv[j].astype(F32)
+        target_rows += trecv[j].astype(F32)
+    whole = rest + jnp.exp(chosen - peak)
+    logp = chosen - peak - jnp.log(whole)
+    reader = jnp.sum(jnp.broadcast_to(logp, (n_pick, 128)).reshape(pairs, slots, 128), 1) / slots
+    joint[0:pairs, :] = reader
+    joint_in[doc, 0:pairs, :] = reader
+    joint_at = net.take(nd)
+    joint_copies = [
+        net.put(joint, joint_in.at[doc], peer, joint_at + j + 1, joint_at + j + 1) for j, peer in enumerate(doc_peers)
+    ]
+    row_grad = (mixture - rest * target_rows) / whole
+
+    for copy in hint_copies:
+        copy.wait_recv()
+    full_query = hints_in[0, 0:pairs, :]
+    for j in range(1, nd):
+        full_query += hints_in[j, 0:pairs, :]
+    docs = [hints_in[j, 8 : 8 + pairs, :] for j in range(nd)]
+    score = [jnp.broadcast_to(jnp.sum(full_query * d, 1, keepdims=True), (pairs, 128)) for d in docs]
+    for copy in joint_copies:
+        copy.wait_recv()
+    both = [s + joint_in[j, 0:pairs, :] for j, s in enumerate(score)]
+
+    def soft(vals):
+        high = vals[0]
+        for v in vals[1:]:
+            high = jnp.maximum(high, v)
+        es = [jnp.exp(v - high) for v in vals]
+        tot = es[0]
+        for e in es[1:]:
+            tot = tot + e
+        return [e / tot for e in es], high + jnp.log(tot)
+
+    w_score, total_score = soft(score)
+    w_joint, total_joint = soft(both)
+    eye = iota((pairs, 128), 0) == iota((pairs, 128), 1)
+    loss_out[...] = jnp.sum(jnp.where(eye, total_score - total_joint, 0.0), 0, keepdims=True)
+    query_grad = (w_score[0] - w_joint[0]) * docs[0]
+    for j in range(1, nd):
+        query_grad += (w_score[j] - w_joint[j]) * docs[j]
+    grad_query[...] = mm_exact(query_grad, spread_lanes, NT)
+    mine = w_joint[0]
+    for j in range(1, nd):
+        mine = jnp.where(doc == j, w_joint[j], mine)
+    row_weight = jnp.broadcast_to(mine.reshape(pairs, 1, 128), (pairs, slots, 128)).reshape(n_pick, 128)[:, 0:1]
+    final_grad = row_grad * (row_weight / slots)
+
+    g1_at, g2_at = net.take(8), net.take(8)
+    g1_send, g2_send = net.take(8), net.take(8)
+    half_w, half_f = width // 2, ff // 2
+
+    def send_right(src, cols, dst, to_core, send_at, recv_at):
+        for k, (dx, dz) in enumerate(sides):
+            peer, tx, _ = side_peer(dx, dz, to_core)
+            part = src.at[:, pl.ds(pl.multiple_of(tx * cols, 128), cols)]
+            land = dst.at[slot, :, pl.ds(0, cols)]
+            args = (part, land, peer, send_at + 2 * k + to_core, recv_at + 2 * k + core)
+            if k:
+                net.put(*args)
+            else:
+                net.put_if(core == 1 - to_core, *args)
+
+                def keep():
+                    dst[slot, :, 0:cols] = src[:, pl.ds(pl.multiple_of(x * cols, 128), cols)]
+
+                pl.when(core == to_core)(keep)
+
+    def wait_right(src, cols, dst, recv_at):
+        part = src.at[:, pl.ds(0, cols)]
+        land = dst.at[slot, :, pl.ds(0, cols)]
+        for k in range(4):
+            for from_core in range(2):
+                i = recv_at + 2 * k + from_core
+                if k:
+                    net.copy(part, land, twin, i, i).wait_recv()
+        i = recv_at + 1 - core
+        net.copy(part, land, twin, i, i).wait_recv()
+
+    vecs[...] = jnp.zeros_like(vecs)
+    sum_grad = norm_back(final_grad, hat2, rstd2, gain2[...])
+    vecs[6:7, :] = jnp.sum(final_grad * hat2, 0, keepdims=True)
+    vecs[7:8, :] = jnp.sum(final_grad, 0, keepdims=True)
+    vecs[5:6, :] = jnp.sum(sum_grad, 0, keepdims=True)
+    second_low = sum_grad.astype(BF16)
+    second_b[...] = second_low
+    send_right(second_b, half_w, g1, 0, g1_send, g1_at)
+    inner_grad = mm_nt(second_low, wdown[...]) * gelu_slope(inner_p)
+    inner_low = inner_grad.astype(BF16)
+    inner_b[...] = inner_low
+    send_right(inner_b, half_f, g1, 1, g1_send, g1_at)
+    up_bias_grad = jnp.sum(inner_grad, 0, keepdims=True)
+    for i in range(ff // width):
+        vecs[8 + i : 9 + i, :] = up_bias_grad[:, i * width : (i + 1) * width]
+    first_grad = sum_grad + mm_nt(inner_low, wup[...])
+    resid_grad = norm_back(first_grad, hat1, rstd1, gain1[...])
+    resid_low = resid_grad.astype(BF16)
+    rest_b[0] = resid_low
+    send_right(rest_b.at[0], half_w, g2, 0, g2_send, g2_at)
+    vecs[3:4, :] = jnp.sum(first_grad * hat1, 0, keepdims=True)
+    vecs[4:5, :] = jnp.sum(first_grad, 0, keepdims=True)
+    vecs[2:3, :] = jnp.sum(resid_grad, 0, keepdims=True)
+    mixed_grad = expand(mm_nt(resid_low, wout[...]).astype(BF16))
+    prob_grad = mm_nt(mixed_grad, vb[...])
+    value_grad = mm_tn(probs_low[...], mixed_grad)
+    p = probs[...]
+    score_low = (p * (prob_grad - jnp.sum(prob_grad * p, -1, keepdims=True)) * scale).astype(BF16)
+    key_grad = mm_tn(score_low, qexp[...])
+    kvb[0] = key_grad.astype(BF16)
+    kvb[1] = value_grad.astype(BF16)
+    kv_at = net.take()
+    kv_copy = net.put(kvb.at[1 - core], kv2.at[pl.ds(rows, rows)], twin, kv_at, kv_at)
+    kv2[0:rows, :] = kvb[core]
+    query_grad_p = fold(mm(score_low, kb[...]))
+    rest_b[1] = query_grad_p.astype(BF16)
+    send_right(rest_b.at[1], half_w, g2, 1, g2_send, g2_at)
+    vecs[0:1, :] = jnp.sum(query_grad_p, 0, keepdims=True)
+    vecs[1:2, :] = jnp.sum(value_grad, 0, keepdims=True)
+
+    runs = []
+    bufs = list(trip_bufs)
+    for t in trips:
+        k = len(t.buffers())
+        runs.append(TripRun(t, bufs[:k], net, spot))
+        bufs = bufs[k:]
+    runs[8].bufs[0][...] = vecs[...].astype(BF16)
+    runs[8].start(0)
+    wait_left()
+    at[0 : 2 * width, :] = a1[...].reshape(8 * n_pick, 2 * width).T
+    at[2 * width : 3 * width, :] = a2[...].reshape(8 * n_pick, width).T
+    quads = [(z1, y) for z1 in range(2) for y in range(2)]
+
+    def block(i, offsets, g, col):
+        left = jnp.concatenate([at[pl.ds(pl.multiple_of(o, 32), share), :] for o in offsets], 0)
+        right = g[:, :, pl.ds(col, half_w)].reshape(8 * n_pick, half_w)
+        out = mm(left, right).astype(BF16)
+        for n, (z1, y) in enumerate(quads):
+            runs[i].bufs[0][z1, y] = out[n * share : (n + 1) * share]
+        runs[i].start(0)
+
+    pl.when(core == 0)(lambda: wait_right(second_b, half_w, g1, g1_at))
+    pl.when(core == 1)(lambda: wait_right(inner_b, half_f, g1, g1_at))
+    for i in range(4):
+        offsets = [
+            (1 - core) * ((2 * z1 + y) * 4 * share + i * share) + core * (4 * z1 + 2 * z0 + y) * share
+            for z1, y in quads
+        ]
+        block(i, offsets, g1, pl.multiple_of(core * i * half_w, 128))
+
+    kv_copy.wait_recv()
+    for j in range(3):
+        right = jnp.concatenate([kv2[:, s * half_w + 128 * j : s * half_w + 128 * (j + 1)] for s in range(2)], 1)
+        out = mm(x2t[...], right).astype(BF16)
+        for s in range(2):
+            for b in range(nb):
+                runs[5 + j].bufs[0][s, b // 4, b // 2 % 2, b % 2] = out[
+                    b * share : (b + 1) * share, 128 * s : 128 * (s + 1)
+                ]
+        runs[5 + j].start(0)
+    wait_right(rest_b.at[0], half_w, g2, g2_at)
+    block(4, [2 * width - width * core + (4 * z1 + 2 * z0 + y) * share for z1, y in quads], g2, 0)
+
+    inward = mm_nt(kvb[0], wqkv[:, width : 2 * width]) + mm_nt(kvb[1], wqkv[:, 2 * width :])
+    at_rows = resid_grad + mm_nt(rest_b[1], wqkv[:, 0:width])
+    grad_in[...] = (inward + mm_exact(pick_f32, at_rows, TN)).astype(BF16)
+
+    ready = [0.0, 0.4, 0.8, 1.2, 5.0, 3.0, 3.5, 4.0, 0.0]
+    for i, step in exchange_order(trips, ready, link_table(8, 4)):
+        runs[i].finish(step)
+        if step + 1 < len(trips[i].steps):
+            runs[i].start(step + 1)
+        elif i < 5:
+            mats_out[i] = runs[i].final[...]
+        elif i < 8:
+            wide_out[i - 5] = runs[i].final[...]
+        else:
+            vec_out[...] = runs[i].final[...]
+    net.drain()
+
+
+def finish_kernel(block, grad, loss, gq, mats, wide, vec, *outs):
+    (o_block, o_loss, o_grad, o_gq, o_qkv, o_qb, o_vb, o_out, o_ob, o_g1, o_s1, o_up, o_ub, o_down, o_db, o_g2, o_s2) = outs
+    batch = lax.axis_index("batch")
+    nb = lax.axis_size("batch")
+    width = vec.shape[1]
+    share, half = width // nb, width // 2
+    o_block[...] = block[...]
+    o_grad[...] = grad[...]
+    o_loss[...] = loss[:, 0 : o_loss.shape[1]]
+    o_gq[...] = gq[...]
+    for s in range(2):
+        cols = slice(s * half, (s + 1) * half)
+        o_out[:, cols] = mats[4, 0, s].astype(F32)
+        o_qkv[:, cols] = mats[4, 1, s].astype(F32)
+        for i in range(4):
+            o_down[i * share : (i + 1) * share, cols] = mats[i, 0, s].astype(F32)
+            o_up[:, (4 * s + i) * half : (4 * s + i + 1) * half] = mats[i, 1, s].astype(F32)
+        for c in range(2):
+            for j in range(3):
+                start = (1 + c) * width + s * half + 128 * j
+                o_qkv[:, start : start + 128] = wide[j, c, s].astype(F32)
+    v = vec[...].astype(F32)
+    take = (iota((width, share), 0) == iota((width, share), 1) + batch * share).astype(F32)
+    got = mm_exact(v, take)
+    for i, o in enumerate((o_qb, o_vb, o_ob, o_g1, o_s1, o_db, o_g2, o_s2)):
+        o[...] = got[i : i + 1, :]
+    side = jnp.where(lax.rem(batch, 2) == 0, v[8:12, 0:half], v[8:12, half:])
+    o_ub[...] = jnp.sum(jnp.where(iota((4, half), 0) == batch // 2, side, 0.0), 0, keepdims=True)
+
+
+def paired_local(*args):
+    (
+        hidden_in, segments, mask_pos, target_ids, query_emb, doc_emb,
+        qkv_weight, query_bias, value_bias, out_weight, out_bias, gain_one, shift_one,
+        up_weight, up_bias, down_weight, down_bias, gain_two, shift_two, vocab,
+    ) = args
+    rows, width = hidden_in.shape[2:]
+    pairs, slots = mask_pos.shape[2:]
+    n_pick = pairs * slots
+    ff = up_weight.shape[1]
+    entries = vocab.shape[0]
+    nb, nd = lax.axis_size("batch"), lax.axis_size("doc")
+    share = width // nb
+    heads = width // HEAD_DIM
+    trips = layer_trips(share)
+    vm, hbm = pl.BlockSpec(memory_space=pltpu.VMEM), pl.BlockSpec(memory_space=pl.ANY)
+
+    def v(shape, dtype=BF16):
+        return pltpu.VMEM(shape, dtype)
+
+    dma = pltpu.SemaphoreType.DMA
+    scratch = [
+        v(qkv_weight.shape), v(out_weight.shape), v(up_weight.shape), v(down_weight.shape), v(vocab.shape),
+        v((rows, width)), v((rows, width)), v((rows, width)), v((rows, width)),
+        v((rows, width), F32), v((rows, width)), v((rows, width), F32),
+        v((2 * rows, width)), v((width, 2 * rows)), v((2, rows, width)), v((2 * rows, width)),
+        v((nb, n_pick, width)), v((nb, n_pick, width)), v((nb, n_pick, width)), v((nb, n_pick, width)),
+        v((nb, n_pick, width)), v((nb, n_pick, 128), F32), v((nb, n_pick, 128), F32), v((nb * n_pick, entries), F32),
+        v((heads * n_pick, width)), v((heads * n_pick, rows), F32), v((heads * n_pick, rows)),
+        v((16, 128), F32), v((nd, 16, 128), F32), v((8, 128), F32), v((nd, 8, 128), F32),
+        v((3, n_pick, 2 * width)), v((n_pick, width)), v((8, n_pick, 2 * width)), v((8, n_pick, width)),
+        v((3 * width, 8 * n_pick)), v((n_pick, width)), v((n_pick, ff)), v((2, n_pick, width)),
+        v((8, n_pick, ff // 2)), v((8, n_pick, width // 2)),
+        v((16, width), F32),
+        dma((6,)), dma((256,)), dma((256,)),
+    ]
+    for t in trips:
+        scratch += [v(shape) for shape in t.buffers()]
+    sds = jax.ShapeDtypeStruct
+    first = pl.pallas_call(
+        partial(layer_kernel, trips),
+        out_shape=[
+            sds((rows, width), BF16),
+            sds((1, 128), F32),
+            sds((rows, width), BF16),
+            sds((pairs, query_emb.shape[2]), F32),
+            sds((5, 2, 2, share, 384), BF16),
+            sds((3, 2, 2, share, 128), BF16),
+            sds((16, width), BF16),
+        ],
+        in_specs=[vm] * 15 + [hbm] * 5,
+        out_specs=[vm] * 7,
+        scratch_shapes=scratch,
+        compiler_params=pltpu.CompilerParams(
+            collective_id=0, has_side_effects=True, vmem_limit_bytes=VMEM_BYTES
+        ),
+        name="layer",
+    )
+    biases = (query_bias, value_bias, out_bias, gain_one, shift_one, up_bias, down_bias, gain_two, shift_two)
+    block, loss, grad, gq, mats, wide, vec = first(
+        hidden_in.reshape(rows, width),
+        segments.reshape(1, rows),
+        mask_pos.reshape(pairs, slots),
+        target_ids,
+        query_emb.reshape(pairs, -1),
+        doc_emb.reshape(pairs, -1),
+        *[b.reshape(1, -1) for b in biases],
+        qkv_weight,
+        out_weight,
+        up_weight,
+        down_weight,
+        vocab,
+    )
+    small = sds((1, share), F32)
+    outs = pl.pallas_call(
+        finish_kernel,
+        out_shape=[
+            sds((rows, width), BF16), sds((1, pairs), F32), sds((rows, width), BF16), sds(gq.shape, F32),
+            sds((share, 3 * width), F32), small, small, sds((share, width), F32), small, small, small,
+            sds((share, ff), F32), sds((1, ff // nb), F32), sds((ff // nb, width), F32), small, small, small,
+        ],
+        in_specs=[vm] * 7,
+        out_specs=[vm] * 17,
+        compiler_params=pltpu.CompilerParams(vmem_limit_bytes=VMEM_BYTES),
+        name="finish",
+    )(block, grad, loss, gq, mats, wide, vec)
+    shapes = [hidden_in.shape, (1, pairs), hidden_in.shape, query_emb.shape]
+    fixed = [o.reshape(s) for o, s in zip(outs[:4], shapes)]
+    return tuple(fixed + [o.reshape(-1) if o.shape[0] == 1 else o for o in outs[4:]])
 
 
 def combined_all(x, axis, combine):
@@ -604,4 +1335,5 @@
         P("batch"),
         P("batch"),
     )
-    return jax.shard_map(local, mesh=mesh, in_specs=in_specs, out_specs=out_specs, check_vma=False)
+    paired = dict(mesh.shape) == {"batch": 8, "doc": 4}
+    return jax.shard_map(paired_local if paired else local, mesh=mesh, in_specs=in_specs, out_specs=out_specs, check_vma=False)

time: 432 us -> 117 us (0.27); the launches traced: 426 us -> 116 us
  blocking collectives: 122 us -> 0 us
  matrix products: 64.4 us -> 0 us
  waiting for transfers between devices: 57.5 us -> 0 us
  other arithmetic: 20.7 us -> 1.27 us
  Pallas kernels: 122 us -> 104 us
  between operations: 16.6 us -> 0.67 us
  local copies, waits for them, and re-layouts: 21.6 us -> 10.2 us
    all_gather x6 -> x0, blocking collectives: 98.3 us -> none  [the longest x4 60.3 us: combined_all(): everything = jax.tree.map(lambda part: lax.all_gather(part, axis), x)]
    dot_general x19 -> x0, matrix products: 58.9 us -> none  [the longest x1 12.6 us: local(): jnp.einsum('nld,df->nlf', first_low, up_weight, preferred_element_type=f32)]
    reduce_scatter x1 -> x0, waiting for transfers between devices: 57.5 us -> none  [local(): lax.psum_scatter(jnp.dot(logit_grad, vocab, preferred_element_type=f32).a...]
    unnamed x2 -> x0, blocking collectives: 24.2 us -> none
    pallas_call x1 -> x2, Pallas kernels: 122 us -> 104 us  [the longest x1 100 us: paired_local(): first(hidden_in.reshape(rows, width), segments.reshape(1, rows), mask_pos...]
    convert_element_type x8 -> x0, other arithmetic: 12 us -> none  [the longest x1 2.94 us: local(): probs_low = probs.astype(bf16)]
    reshape x4 -> x8, local copies, waits for them, and re-layouts: 0.19 us -> 10.2 us  [paired_local(): b.reshape(1, -1)]
    unnamed x104 -> x0, local copies, waits for them, and re-layouts: 9.06 us -> none
  transfers between devices with their start and end apart: 2 -> 0, of which waited for: 1 -> 0; matrix products, arithmetic and copies ran while one was open for 1% -> 0% of each run, Pallas kernels for 0% -> 0%
where the time goes in v1:
time: 117 us; the launch traced here: 116 us
  Pallas kernels  104 us (89%)
  local copies, waits for them, and re-layouts  10.2 us (9%)
  other arithmetic  1.27 us (1%)
    pallas_call x1, Pallas kernels, paired_local(): first(hidden_in.reshape(rows, width), segments.reshape(1, rows), mask_pos...  100 us
    reshape x8, local copies, waits for them, and re-layouts, paired_local(): b.reshape(1, -1)  10.2 us
    pallas_call x1, Pallas kernels, paired_local(): pl.pallas_call(finish_kernel, out_shape=[sds((rows, width), BF16), sds((1...  4.13 us

profile of v1, /device:TPU:0, one launch (start us, length us, event | category | flops | bytes accessed | tf_op | source)
XLA Modules:
  0.0 116.3 jit_solution(12682746425782281994)
XLA Ops:
  0.7 1.3 %reshape.117.refs_6_ = f32[1,768]{1,0:T(1,128)} reshape(f32[768]{0:T(1024)} %param.27) | data formatting | bytes 6144 | tf_op jit(solution)/shard_map/reshape | solution.py:1019
  1.9 1.3 %reshape.118.refs_7_ = f32[1,768]{1,0:T(1,128)} reshape(f32[768]{0:T(1024)} %param.28) | data formatting | bytes 6144 | tf_op jit(solution)/shard_map/reshape | solution.py:1019
  3.2 1.3 %reshape.119.refs_8_ = f32[1,768]{1,0:T(1,128)} reshape(f32[768]{0:T(1024)} %param.30) | data formatting | bytes 6144 | tf_op jit(solution)/shard_map/reshape | solution.py:1019
  4.5 1.3 %reshape.120.refs_9_ = f32[1,768]{1,0:T(1,128)} reshape(f32[768]{0:T(1024)} %param.31) | data formatting | bytes 6144 | tf_op jit(solution)/shard_map/reshape | solution.py:1019
  5.7 1.3 %reshape.121.refs_10_ = f32[1,768]{1,0:T(1,128)} reshape(f32[768]{0:T(1024)} %param.32) | data formatting | bytes 6144 | tf_op jit(solution)/shard_map/reshape | solution.py:1019
  7.0 1.3 %reshape.123.refs_12_ = f32[1,768]{1,0:T(1,128)} reshape(f32[768]{0:T(1024)} %param.36) | data formatting | bytes 6144 | tf_op jit(solution)/shard_map/reshape | solution.py:1019
  8.3 1.3 %reshape.124.refs_13_ = f32[1,768]{1,0:T(1,128)} reshape(f32[768]{0:T(1024)} %param.37) | data formatting | bytes 6144 | tf_op jit(solution)/shard_map/reshape | solution.py:1019
  9.5 1.3 %reshape.125.refs_14_ = f32[1,768]{1,0:T(1,128)} reshape(f32[768]{0:T(1024)} %param.38) | data formatting | bytes 6144 | tf_op jit(solution)/shard_map/reshape | solution.py:1019
  10.8 100.1 %layer.1 = (bf16[288,768]{1,0:T(8,128)(2,1)}, f32[1,128]{1,0:T(1,128)}, bf16[288,768]{1,0:T(8,128)(2,1)}, f32[4,32]{1,0:T(4,128)}, bf16[5,2,2,96,384]{4,3,2,1,0:...) custom-call(bf16[288,768]{1,0:T(8,128)(2,1)} %bitcast.17, s32[1,288]{1,0:T(1,128)} %bitcast.22, ...), custom_call_target="tpu_custom_call" | custom-call | tf_op jit(solution)/shard_map/layer/pallas_call | solution.py:1012
  110.9 4.1 %finish.1 = (bf16[288,768]{1,0:T(8,128)(2,1)}, f32[1,4]{1,0:T(1,128)}, bf16[288,768]{1,0:T(8,128)(2,1)}, f32[4,32]{1,0:T(4,128)}, f32[96,2304]{1,0:T(8,128)}, /*...) custom-call(bf16[288,768]{1,0:T(8,128)(2,1)} %get-tuple-element.41.b, ...), custom_call_target="tpu_custom_call" | custom-call | tf_op jit(solution)/shard_map/finish/pallas_call | solution.py:1027
  115.0 1.3 %reduce = f32[384]{0:T(512)} reduce(f32[1,384]{1,0:T(1,128)} %get-tuple-element.60, f32[]{:T(128)} %constant.5), dimensions={0}, to_apply=%get-tuple-element.60.reduce_sub_computation | reduce | bytes 3076 | tf_op jit(solution)/shard_map/finish/pallas_call | solution.py:1027

commit v2 on v1

--- a/solution.py
+++ b/solution.py
@@ -21,6 +21,10 @@
     def mine(self, key):
         axis, k = key
         return lax.rem(self.at[axis] // (1 << k), 2)
+
+    def others(self):
+        nd = lax.axis_size("doc")
+        return [(self.at["batch"], lax.rem(self.at["doc"] + j, nd)) for j in range(1, nd)]
 
     def peer(self, key):
         axis, k = key
@@ -369,70 +373,80 @@
 
 class Net:
     def __init__(self, send, recv):
-        self.send, self.recv, self.used, self.open = send, recv, 0, []
-
-    def take(self, n=1):
-        self.used += n
-        return self.used - n
-
-    def copy(self, src, dst, peer, send_at, recv_at):
+        self.send, self.recv, self.sends, self.recvs, self.open, self.due = send, recv, 0, 0, [], {}
+
+    def branch(self):
+        twin = Net(self.send, self.recv)
+        twin.open = list(self.open)
+        twin.due = {k: list(v) for k, v in self.due.items()}
+        return twin
+
+    def take(self):
+        self.sends += 1
+        self.recvs += 1
+        return self.sends - 1, self.recvs - 1
+
+    def copy(self, src, dst, peer, at):
         return pltpu.make_async_remote_copy(
             src_ref=src,
             dst_ref=dst,
-            send_sem=self.send.at[send_at],
-            recv_sem=self.recv.at[recv_at],
+            send_sem=self.send.at[at[0]],
+            recv_sem=self.recv.at[at[1]],
             device_id=peer,
             device_id_type=MESH,
         )
 
-    def put(self, src, dst, peer, send_at, recv_at):
-        copy = self.copy(src, dst, peer, send_at, recv_at)
-        copy.start()
-        self.open.append((None, copy))
-        return copy
-
-    def put_if(self, cond, src, dst, peer, send_at, recv_at):
-        copy = self.copy(src, dst, peer, send_at, recv_at)
-        pl.when(cond)(copy.start)
-        self.open.append((cond, copy))
-        return copy
+    def put(self, src, dst, peer, at):
+        self.copy(src, dst, peer, at).start()
+
+    def group(self, due, copies, whole):
+        at = self.take()
+        for src, dst, peer in copies:
+            self.put(src, dst, peer, at)
+        all_of = self.copy(whole(len(copies)), whole(len(copies)), copies[0][2], at)
+        self.expect(due, all_of.wait_recv)
+        self.open.append(all_of.wait_send)
+
+    def expect(self, due, wait):
+        self.due.setdefault(due, []).append(wait)
+
+    def collect(self, due):
+        for wait in self.due.pop(due):
+            wait()
 
     def drain(self):
-        for cond, copy in self.open:
-            if cond is None:
-                copy.wait_send()
-            else:
-                pl.when(cond)(copy.wait_send)
+        for wait in self.open:
+            wait()
         self.open = []
 
 
 class Trip:
-    def __init__(self, tile, lead, halve, both, spread, twin):
+    def __init__(self, tile, lead, halve, both, end):
         self.tile, self.lead, self.halve, self.both = tile, lead, halve, both
         self.steps = [("halve", k) for k in halve] + [("both", k) for k in both]
         self.sums = len(self.steps)
-        self.steps += [("spread", k) for k in spread] + ([("twin", ("doc", 0))] if twin else [])
-        self.spread, self.twin = spread, twin
+        ends = {"": [], "two": [("spread", ("doc", 1)), ("twin", ("doc", 0))], "three": [("three", None)]}
+        self.steps += ends[end]
+        self.end = end
 
     def buffers(self):
         shapes = [(2,) * len(self.lead) + self.tile]
         shapes += [(2,) * (len(self.lead) - i - 1) + self.tile for i in range(len(self.halve))]
         shapes += [self.tile] * len(self.both)
-        return shapes + [(2,) * (self.twin + len(self.spread)) + self.tile]
+        return shapes + [((2, 2) if self.end else ()) + self.tile]
 
     def bytes(self, i):
         kind, key = self.steps[i]
         unit = 2 * math.prod(self.tile)
         if kind == "halve":
             return unit * 2 ** (len(self.lead) - i - 1)
-        return unit * (2 ** len(self.spread) if kind == "twin" else 1)
+        return unit * {"twin": 2, "three": 2}.get(kind, 1)
 
 
 class TripRun:
-    def __init__(self, trip, bufs, net, spot):
-        self.t, self.bufs, self.net, self.spot = trip, bufs, net, spot
-        self.base = net.take(len(trip.steps))
-        self.live, self.copies = {}, []
+    def __init__(self, trip, bufs, sems, net, spot):
+        self.t, self.bufs, self.at_step, self.net, self.spot = trip, bufs, sems, net, spot
+        self.live = {}
 
     @property
     def final(self):
@@ -442,12 +456,22 @@
         return tuple(fixed.get(key, slice(None)) for key in self.t.lead)
 
     def place(self):
-        return ((self.spot.mine(("doc", 0)),) if self.t.twin else ()) + tuple(
-            self.spot.mine(k) for k in self.t.spread
-        )
+        return (self.spot.mine(("doc", 0)), self.spot.mine(("doc", 1))) if self.t.end else ()
 
     def start(self, step):
         kind, key = self.t.steps[step]
+        if kind == "three":
+            mine = self.final.at[self.place()]
+            sem = self.at_step[step]
+            for peer in self.spot.others():
+                self.net.put(mine, mine, peer, sem)
+            pair, one = self.final.at[0], self.final.at[0, 0]
+            peer = self.spot.peer(("doc", 0))
+            for view in (pair, one):
+                copy = self.net.copy(view, view, peer, sem)
+                self.net.expect(sem, copy.wait_recv)
+                self.net.open.append(copy.wait_send)
+            return
         if kind == "halve":
             src = self.bufs[0].at[self.at({**self.live, key: 1 - self.spot.mine(key)})]
             dst = self.bufs[1 + step]
@@ -457,19 +481,18 @@
             src = dst = self.final.at[self.place()]
         else:
             src = dst = self.final.at[self.spot.mine(key)]
-        at = self.base + step
-        copy = self.net.copy(src, dst, self.spot.peer(key), at, at)
+        at = self.at_step[step]
+        copy = self.net.copy(src, dst, self.spot.peer(key), at)
         copy.start()
-        self.copies.append(copy)
+        self.net.expect(at, copy.wait_recv)
+        if kind == "both":
+            self.net.expect(at, copy.wait_send)
+        else:
+            self.net.open.append(copy.wait_send)
 
     def finish(self, step):
         kind, key = self.t.steps[step]
-        copy = self.copies[step]
-        copy.wait_recv()
-        if kind == "both":
-            copy.wait_send()
-        else:
-            self.net.open.append((None, copy))
+        self.net.collect(self.at_step[step])
         if step < self.t.sums:
             if kind == "halve":
                 self.live[key] = self.spot.mine(key)
@@ -484,12 +507,66 @@
                     self.bufs[0][at] = total
 
 
+ALONG_Z = 2
+
+
 def layer_trips(share):
     y, z0, z1, x = ("batch", 0), ("batch", 1), ("batch", 2), ("doc", 1)
-    block = [Trip((share, 384), [z1, y], [y, z1], [], [x], True) for _ in range(5)]
-    wide = [Trip((share, 128), [x, z1, z0, y], [x, y, z0, z1], [], [x], True) for _ in range(3)]
-    small = Trip((16, 768), [], [], [y, z0, z1, x, ("doc", 0)], [], False)
+    block = [Trip((share, 384), [z1, y], [y, z1], [], "two") for _ in range(ALONG_Z)]
+    block += [Trip((share, 384), [z1, z0], [z0, z1], [], "two") for _ in range(4 - ALONG_Z)]
+    block += [Trip((share, 384), [z1, y], [y, z1], [], "two")]
+    orders = [[y, z0, z1], [y, z0, z1], [y, z0, z1]]
+    wide = [Trip((share, 128), [z1, z0, y], order, [], "two") for order in orders]
+    small = Trip((16, 768), [], [], [y, z0, z1, x, ("doc", 0)], "")
     return block + wide + [small]
+
+
+LINKS = {
+    ("batch", 0): [("y", 2.0)],
+    ("batch", 1): [("z", 2.0)],
+    ("batch", 2): [("far", 4.0), ("z", 2.0)],
+    ("doc", 1): [("x", 2.0)],
+    ("doc", 0): [("twin", 0.2)],
+    None: [("x", 2.0)],
+}
+IN_FLIGHT = 2
+LINK_RATE = 91e3
+
+
+def trip_program(trips, stages):
+    def wire(i, step):
+        uses = LINKS[trips[i].steps[step][1]]
+        return [(link, trips[i].bytes(step) * copies / LINK_RATE) for link, copies in uses]
+
+    def to_go(i, step):
+        return sum(max(t for _, t in wire(i, n)) + 2.0 for n in range(step, len(trips[i].steps)))
+
+    events = [(at, -1, n, 0) for n, (at, _) in enumerate(stages)]
+    free, flying, waiting, program = {}, {}, {}, []
+    while events:
+        events.sort()
+        now, kind, i, step = events.pop(0)
+        if kind < 0:
+            program.append(("make", i, 0))
+            ready = [(n, 0) for n in stages[i][1]]
+        else:
+            program.append(("finish", i, step))
+            flying[wire(i, step)[0][0]] -= 1
+            ready = [(i, step + 1)] if step + 1 < len(trips[i].steps) else []
+        for n, s in ready:
+            waiting.setdefault(wire(n, s)[0][0], []).append((-to_go(n, s), n, s))
+        for link, queue in waiting.items():
+            while queue and flying.get(link, 0) < IN_FLIGHT:
+                queue.sort()
+                _, n, s = queue.pop(0)
+                program.append(("start", n, s))
+                flying[link] = flying.get(link, 0) + 1
+                end = now
+                for used, t in wire(n, s):
+                    free[used] = max(now, free.get(used, 0.0)) + t
+                    end = max(end, free[used])
+                events.append((end + 1.8, 0, n, s))
+    return program
 
 
 def layer_kernel(trips, *refs):
@@ -500,14 +577,18 @@
         block_out, loss_out, grad_in, grad_query, mats_out, wide_out, vec_out,
         wqkv, wout, wup, wdown, wvoc,
         qb, kb, vb, mixed, first_norm, first_low, acc,
-        x2, x2t, kvb, kv2,
-        picks, tsend, trecv, usend, urecv, ssend, srecv, logits,
+        x4, x4t, kvb, kv4, sp, sp_send, qm, qm_send,
+        picks, tsend, trecv, target_rows, usend, urecv, ssend, srecv, logits,
         qexp, probs, probs_low,
         hints, hints_in, joint, joint_in,
-        a_send, a_mixed, a1, a2, at, second_b, inner_b, rest_b, g1, g2,
-        vecs,
+        left0, left0_y, left1, left1_y, a1, a1_y, at, at_y, second_b, inner_b, rest_b, g1, g1_y, g2,
+        vecs, up_bias_s,
         load_sem, send, recv, *trip_bufs,
     ) = refs
+    bias_q, bias_v, bias_o, gain1, shift1, bias_up, bias_down, gain2, shift2 = (
+        b[...].reshape(1, -1) for b in (bias_q, bias_v, bias_o, gain1, shift1, bias_up, bias_down, gain2, shift2)
+    )
+    left0, left1, a1, at, g1 = (left0, left0_y), (left1, left1_y), (a1, a1_y), (at, at_y), (g1, g1_y)
     spot = Spot()
     batch, doc = spot.at["batch"], spot.at["doc"]
     nb, nd = lax.axis_size("batch"), lax.axis_size("doc")
@@ -522,25 +603,61 @@
 
     loads = [
         pltpu.make_async_copy(qkv_hbm.at[:, pl.ds(width, 2 * width)], wqkv.at[:, pl.ds(width, 2 * width)], load_sem.at[0]),
-        pltpu.make_async_copy(qkv_hbm.at[:, pl.ds(0, width)], wqkv.at[:, pl.ds(0, width)], load_sem.at[1]),
-        pltpu.make_async_copy(out_hbm, wout, load_sem.at[2]),
-        pltpu.make_async_copy(up_hbm, wup, load_sem.at[3]),
-        pltpu.make_async_copy(down_hbm, wdown, load_sem.at[4]),
-        pltpu.make_async_copy(vocab_hbm, wvoc, load_sem.at[5]),
+        pltpu.make_async_copy(vocab_hbm, wvoc, load_sem.at[1]),
+        pltpu.make_async_copy(qkv_hbm.at[:, pl.ds(0, width)], wqkv.at[:, pl.ds(0, width)], load_sem.at[2]),
+        pltpu.make_async_copy(out_hbm, wout, load_sem.at[3]),
+        pltpu.make_async_copy(up_hbm, wup, load_sem.at[4]),
+        pltpu.make_async_copy(down_hbm, wdown, load_sem.at[5]),
     ]
     for load in loads:
         load.start()
 
     batch_peers = [(lax.rem(batch + j, nb), doc) for j in range(1, nb)]
     doc_peers = [(batch, lax.rem(doc + j, nd)) for j in range(1, nd)]
-    sides = [(dx, dz) for dz in range(2) for dx in range(2)]
-
-    def side_peer(dx, dz, to_core):
+
+    def side_peer(dx, dz, to_core, key):
         tx = lax.rem(x + dx, 2)
-        tz = lax.rem(z0 + dz, 2)
-        return (batch + 2 * (tz - z0), 2 * tx + to_core), tx, tz
-
-    far = [side_peer(1, 1, core)[0], side_peer(1, 1, 1 - core)[0], side_peer(0, 1, 1 - core)[0]]
+        mine = spot.mine(key)
+        tz = lax.rem(mine + dz, 2)
+        return (batch + (tz - mine) * (1 << key[1]), 2 * tx + to_core), tx, tz
+
+    routes = [("batch", 1), ("batch", 0)]
+    twin = spot.peer(("doc", 0))
+    slots_of = [4 * spot.mine(key) + doc for key in routes]
+
+    def fan(due, part_of, dst, lanes, to_core, dzs, route):
+        slot = slots_of[route]
+        sem = net.take()
+        land = dst.at[slot, :, pl.ds(0, lanes)]
+        always = 0
+        for dz in dzs:
+            for dx in range(2):
+                peer, tx, tz = side_peer(dx, dz, to_core, routes[route])
+                copy = net.copy(part_of(tx, tz), land, peer, sem)
+                if dx or dz:
+                    copy.start()
+                    always += 1
+                else:
+                    pl.when(core != to_core)(copy.start)
+        own = 0 in dzs
+
+        def sized(n):
+            view = dst.at[pl.ds(0, n), :, pl.ds(0, lanes)]
+            return net.copy(view, view, twin, sem)
+
+        def sent():
+            if own:
+                pl.when(core != to_core)(sized(always + 1).wait_send)
+                pl.when(core == to_core)(sized(always).wait_send)
+            else:
+                sized(always).wait_send()
+
+        net.open.append(sent)
+        net.expect(due, lambda: pl.when(core == to_core)(sized(4 * len(dzs) - own).wait_recv))
+
+    far = [
+        side_peer(dx, 1, lax.rem(core + dc, 2), key)[0] for key in routes for dx, dc in ((1, 0), (1, 1), (0, 1))
+    ]
     everyone = batch_peers + doc_peers + far
     barrier = pltpu.get_barrier_semaphore()
     for peer in everyone:
@@ -553,14 +670,11 @@
     hints[8 : 8 + pairs, :] = doc_rows[...]
     hints_in[doc, 0:pairs, :] = hints[0:pairs, :]
     hints_in[doc, 8 : 8 + pairs, :] = hints[8 : 8 + pairs, :]
-    hint_at = net.take(nd)
-    hint_copies = [
-        net.put(hints, hints_in.at[doc], peer, hint_at + j + 1, hint_at + j + 1) for j, peer in enumerate(doc_peers)
-    ]
-    twin = spot.peer(("doc", 0))
-    x2_at = net.take()
-    x2_copy = net.put(hidden, x2.at[pl.ds(rows, rows)], twin, x2_at, x2_at)
-    x2[0:rows, :] = hidden[...]
+    net.group("hint", [(hints, hints_in.at[doc], peer) for peer in doc_peers], lambda n: hints_in.at[pl.ds(0, n)])
+    beside = spot.peer(("doc", 1))
+    net.group("tokens", [(hidden, x4.at[doc], beside)], lambda n: x4.at[pl.ds(0, n)])
+    net.group("all tokens", [(hidden, x4.at[doc], twin)], lambda n: x4.at[pl.ds(0, n)])
+    x4[doc] = hidden[...]
 
     place_col = column_of(places[...])
     pick_bool = iota((n_pick, rows), 1) == place_col
@@ -569,10 +683,20 @@
     tokens = hidden[...]
     loads[0].wait()
     kb[...] = mm(tokens, wqkv[:, width : 2 * width]).astype(BF16)
-    vb[...] = (mm(tokens, wqkv[:, 2 * width :]) + bias_v[...]).astype(BF16)
+    vb[...] = (mm(tokens, wqkv[:, 2 * width :]) + bias_v).astype(BF16)
     tokens_p = mm(pick, tokens).astype(BF16)
+
     loads[1].wait()
-    query_p = (mm(tokens_p, wqkv[:, 0:width]) + bias_q[...]).astype(BF16)
+    entries = wvoc.shape[0]
+    target_col = jnp.concatenate([column_of(targets[j]) for j in range(nb)], 0) - batch * entries
+    all_rows = nb * n_pick
+    is_target = iota((all_rows, entries), 1) == target_col
+    tsend[...] = mm(is_target.astype(BF16), wvoc[...]).astype(BF16).reshape(nb, nd, n_pick // nd, width)
+    trecv[batch] = tsend[batch, doc]
+    net.group("part", [(tsend.at[p[0], doc], trecv.at[batch], p) for p in batch_peers], lambda n: trecv.at[pl.ds(0, n)])
+
+    loads[2].wait()
+    query_p = (mm(tokens_p, wqkv[:, 0:width]) + bias_q).astype(BF16)
 
     tall = heads * n_pick
     own_head = iota((tall, width), 0) // n_pick == iota((tall, width), 1) // HEAD_DIM
@@ -596,78 +720,99 @@
     probs[...] = weights
     probs_low[...] = weights.astype(BF16)
     mixed_p = fold(mm(probs_low[...], vb[...])).astype(BF16)
-    loads[2].wait()
-    attended = mm(mixed_p, wout[...]) + bias_o[...]
+    loads[3].wait()
+    attended = mm(mixed_p, wout[...]) + bias_o
     hat1, rstd1 = normed(tokens_p.astype(F32) + attended)
-    first_p = hat1 * gain1[...] + shift1[...]
+    first_p = hat1 * gain1 + shift1
     first_low_p = first_p.astype(BF16)
-    loads[3].wait()
-    inner_p = mm(first_low_p, wup[...]) + bias_up[...]
+    loads[4].wait()
+    inner_p = mm(first_low_p, wup[...]) + bias_up
     active_p = gelu(inner_p).astype(BF16)
-    loads[4].wait()
-    second_p = mm(active_p, wdown[...]) + bias_down[...]
+    loads[5].wait()
+    second_p = mm(active_p, wdown[...]) + bias_down
     hat2, rstd2 = normed(first_p + second_p)
-    picks[batch] = (hat2 * gain2[...] + shift2[...]).astype(BF16)
-    pick_at = net.take(nb)
-    pick_copies = [
-        net.put(picks.at[batch], picks.at[batch], peer, pick_at + j + 1, pick_at + j + 1)
-        for j, peer in enumerate(batch_peers)
-    ]
+    picks[batch] = (hat2 * gain2 + shift2).astype(BF16)
+    net.group("pick", [(picks.at[batch], picks.at[batch], p) for p in batch_peers], lambda n: picks.at[pl.ds(0, n)])
 
     ff = wup.shape[1]
-    for k in range(2):
-        for half in range(2):
-            start = (2 * half + k) * 2 * (ff // nb)
-            a_send[k, :, half * width : (half + 1) * width] = active_p[:, start : start + width]
-    a_send[2, :, 0:width] = first_low_p
-    a_send[2, :, width : 2 * width] = tokens_p
-    a_mixed[...] = mixed_p
-    slot = 4 * z0 + doc
-    a1_at, a2_at = net.take(8), net.take(8)
-    a1[slot] = a_send[(1 - core) * z0 + 2 * core]
-    a2[slot] = a_mixed[...]
-
-    def send_left(k):
-        dx, dz = sides[k]
-        for other in range(2):
-            if k == 0 and other == 0:
-                continue
-            to_core = core if other == 0 else 1 - core
-            peer, tx, tz = side_peer(dx, dz, to_core)
-            part = a_send.at[(1 - to_core) * tz + 2 * to_core]
-            net.put(part, a1.at[slot], peer, a1_at + 2 * k + other, a1_at + 2 * k + other)
-            net.put(a_mixed, a2.at[slot], peer, a2_at + 2 * k + other, a2_at + 2 * k + other)
-
-    def wait_left():
-        for k in range(4):
-            for other in range(2):
-                if k or other:
-                    i = 2 * k + other
-                    net.copy(a_send.at[0], a1.at[slot], twin, a1_at + i, a1_at + i).wait_recv()
-                    net.copy(a_mixed, a2.at[slot], twin, a2_at + i, a2_at + i).wait_recv()
-
-    send_left(0)
-    send_left(1)
-
-    loads[5].wait()
-    entries = wvoc.shape[0]
-    target_col = jnp.concatenate([column_of(targets[j]) for j in range(nb)], 0) - batch * entries
-    all_rows = nb * n_pick
-    is_target = iota((all_rows, entries), 1) == target_col
-    tsend[...] = mm(is_target.astype(BF16), wvoc[...]).astype(BF16).reshape(nb, n_pick, width)
-    trecv[batch] = tsend[batch]
-    t_at = net.take(nb)
-    t_copies = [
-        net.put(tsend.at[peer[0]], trecv.at[batch], peer, t_at + j + 1, t_at + j + 1)
-        for j, peer in enumerate(batch_peers)
-    ]
+    counts = [ALONG_Z, 4 - ALONG_Z]
+    firsts = [0, ALONG_Z]
+    quads = [(z1, other) for z1 in range(2) for other in range(2)]
+    lanes0 = [4 * share * (counts[0] + 1), 4 * share * counts[1]]
+    lanes1 = [8 * share, 4 * share]
+    for route in range(2):
+        wide_lanes = share * counts[route]
+        for k in range(2):
+            for n, (z1, other) in enumerate(quads):
+                b = 4 * z1 + (2 * k + other if route == 0 else 2 * other + k)
+                own = slice(b * share, (b + 1) * share)
+                start = 4 * share * b + share * firsts[route]
+                left0[route][k, :, n * wide_lanes : (n + 1) * wide_lanes] = active_p[:, start : start + wide_lanes]
+                left1[route][k, :, n * share : (n + 1) * share] = first_low_p[:, own]
+                if route == 0:
+                    at0 = 4 * wide_lanes + n * share
+                    left0[route][k, :, at0 : at0 + share] = mixed_p[:, own]
+                    left1[route][k, :, (4 + n) * share : (5 + n) * share] = tokens_p[:, own]
+
+    def keep_left(route, left, lanes):
+        def keep():
+            a1[route][slots_of[route], :, 0:lanes] = left[route][spot.mine(routes[route])]
+
+        return keep
+
+    for route in range(2):
+        pl.when(core == 0)(keep_left(route, left0, lanes0[route]))
+        pl.when(core == 1)(keep_left(route, left1, lanes1[route]))
+
+    def send_left(dzs):
+        for route in range(2):
+            fan("left", lambda tx, tz: left0[route].at[tz], a1[route], lanes0[route], 0, dzs, route)
+            fan("left", lambda tx, tz: left1[route].at[tz], a1[route], lanes1[route], 1, dzs, route)
+
+    half_w, half_f = width // 2, ff // 2
+    tall_half = tall // 2
+    send_left([0])
+
+    def half_heads(due, src, dst, to_core):
+        sem = net.take()
+        for dx in range(2):
+            peer, tx, _ = side_peer(dx, 0, to_core, routes[0])
+            copy = net.copy(src.at[tx], dst.at[doc], peer, sem)
+            if dx:
+                copy.start()
+            else:
+                pl.when(core != to_core)(copy.start)
+
+        def keep():
+            dst[doc] = src[x]
+
+        def sized(n):
+            view = dst.at[pl.ds(0, n)]
+            return net.copy(view, view, twin, sem)
+
+        def sent():
+            pl.when(core != to_core)(sized(2).wait_send)
+            pl.when(core == to_core)(sized(1).wait_send)
+
+        pl.when(core == to_core)(keep)
+        net.open.append(sent)
+        net.expect(due, lambda: pl.when(core == to_core)(sized(3).wait_recv))
+
+    def halves(dst, v):
+        for s in range(2):
+            dst[s] = v[:, s * half_w : (s + 1) * half_w]
+
+    sp_send[1] = probs_low[...].reshape(2, tall_half, rows)
+    half_heads("heads", sp_send.at[1], sp, 1)
+    halves(qm_send.at[0], query_p)
+    half_heads("heads", qm_send.at[0], qm, 0)
 
     seg_col = jnp.sum(
         jnp.where(iota((rows, rows), 0) == iota((rows, rows), 1), jnp.broadcast_to(seg_row, (rows, rows)), 0),
         1,
         keepdims=True,
     )
-    qb[...] = (mm(tokens, wqkv[:, 0:width]) + bias_q[...]).astype(BF16)
+    qb[...] = (mm(tokens, wqkv[:, 0:width]) + bias_q).astype(BF16)
 
     def attend(i):
         lanes = pl.ds(pl.multiple_of(i * 128, 128), 128)
@@ -683,10 +828,20 @@
             parts.append(mm(p, v_s))
         mixed[:, lanes] = jnp.where(low, parts[0], parts[1]).astype(BF16)
 
-    pl.loop(0, width // 128)(attend)
-
-    for copy in pick_copies:
-        copy.wait_recv()
+    half_way = width // 256
+    pl.loop(0, half_way)(attend)
+    send_left([1])
+    net.collect("tokens")
+    net.group("all tokens", [(x4.at[beside[1]], x4.at[beside[1]], twin)], lambda n: x4.at[pl.ds(0, n)])
+    net.collect("part")
+    part = trecv[0].astype(F32)
+    for j in range(1, nb):
+        part += trecv[j].astype(F32)
+    target_rows[doc] = part.astype(BF16)
+    net.group("target", [(target_rows.at[doc], target_rows.at[doc], p) for p in doc_peers], lambda n: target_rows.at[pl.ds(0, n)])
+    pl.loop(half_way, width // 128)(attend)
+
+    net.collect("pick")
     logits[...] = mm_nt(picks[...].reshape(all_rows, width), wvoc[...])
     lg = logits[...]
     top = jnp.max(lg, 1, keepdims=True)
@@ -694,74 +849,65 @@
     others = jnp.where(is_target, 0.0, jnp.exp(lg - top))
     total = jnp.sum(others, 1, keepdims=True)
     lane = iota((all_rows, 128), 1)
-    stats = jnp.where(lane == 0, top, jnp.where(lane == 1, total, chosen))
-    ssend[...] = stats.reshape(nb, n_pick, 128)
+    stats = jnp.where(lane == 0, top, jnp.where(lane == 1, total, chosen)).T
+    blank = jnp.zeros((8, 128 - n_pick), F32)
+    for j in range(nb):
+        ssend[j] = jnp.concatenate([stats[0:8, n_pick * j : n_pick * (j + 1)], blank], 1)
+    srecv[batch] = ssend[batch]
+    net.group("stats", [(ssend.at[p[0]], srecv.at[batch], p) for p in batch_peers], lambda n: srecv.at[pl.ds(0, n)])
     usend[...] = mm(others.astype(BF16), wvoc[...]).astype(BF16).reshape(nb, n_pick, width)
-    srecv[batch] = ssend[batch]
     urecv[batch] = usend[batch]
-    s_at, u_at = net.take(nb), net.take(nb)
-    s_copies, u_copies = [], []
-    for j, peer in enumerate(batch_peers):
-        s_copies.append(net.put(ssend.at[peer[0]], srecv.at[batch], peer, s_at + j + 1, s_at + j + 1))
-        u_copies.append(net.put(usend.at[peer[0]], urecv.at[batch], peer, u_at + j + 1, u_at + j + 1))
+    net.group("back", [(usend.at[p[0]], urecv.at[batch], p) for p in batch_peers], lambda n: urecv.at[pl.ds(0, n)])
 
     tokens = hidden[...]
-    hat, _ = normed(tokens.astype(F32) + mm(mixed[...], wout[...]) + bias_o[...])
-    first_norm[...] = hat * gain1[...] + shift1[...]
+    hat, _ = normed(tokens.astype(F32) + mm(mixed[...], wout[...]) + bias_o)
+    first_norm[...] = hat * gain1 + shift1
     first_low[...] = first_norm[...].astype(BF16)
-    acc[...] = first_norm[...] + bias_down[...]
+    acc[...] = first_norm[...] + bias_down
     chunk = 512
+    up_bias_s[...] = bias_up
 
     def feed(i):
         cols = pl.ds(pl.multiple_of(i * chunk, chunk), chunk)
-        hid = mm(first_low[...], wup[:, cols]) + bias_up[:, cols]
+        hid = mm(first_low[...], wup[:, cols]) + up_bias_s[:, cols]
         acc[...] += mm(gelu(hid).astype(BF16), wdown[cols, :])
 
-    pl.loop(0, ff // chunk)(feed)
-    hat, _ = normed(acc[...])
-    block_out[...] = (hat * gain2[...] + shift2[...]).astype(BF16)
-    x2_copy.wait_recv()
-    x2t[...] = x2[...].T
-
-    for group in (s_copies, t_copies, u_copies):
-        for copy in group:
-            copy.wait_recv()
-    send_left(2)
-    send_left(3)
-    tops = [srecv[j][:, 0:1] for j in range(nb)]
+    pl.loop(0, ff // chunk // 2)(feed)
+
+    net.collect("stats")
+    tops = [srecv[j][0:1, :] for j in range(nb)]
     peak = tops[0]
     for t in tops[1:]:
         peak = jnp.maximum(peak, t)
+    factors = [jnp.exp(t - peak) for t in tops]
     rest = jnp.zeros_like(peak)
     chosen = jnp.zeros_like(peak)
-    mixture = jnp.zeros((n_pick, width), F32)
-    target_rows = jnp.zeros((n_pick, width), F32)
     for j in range(nb):
-        factor = jnp.exp(tops[j] - peak)
-        rest += factor * srecv[j][:, 1:2]
-        chosen += srecv[j][:, 2:3]
-        mixture += factor * urecv[j].astype(F32)
-        target_rows += trecv[j].astype(F32)
+        rest += factors[j] * srecv[j][1:2, :]
+        chosen += srecv[j][2:3, :]
     whole = rest + jnp.exp(chosen - peak)
     logp = chosen - peak - jnp.log(whole)
-    reader = jnp.sum(jnp.broadcast_to(logp, (n_pick, 128)).reshape(pairs, slots, 128), 1) / slots
-    joint[0:pairs, :] = reader
-    joint_in[doc, 0:pairs, :] = reader
-    joint_at = net.take(nd)
-    joint_copies = [
-        net.put(joint, joint_in.at[doc], peer, joint_at + j + 1, joint_at + j + 1) for j, peer in enumerate(doc_peers)
-    ]
-    row_grad = (mixture - rest * target_rows) / whole
-
-    for copy in hint_copies:
-        copy.wait_recv()
+    of_pair = iota((pairs, 128), 1) // slots == iota((pairs, 128), 0)
+    reader = jnp.sum(jnp.where(of_pair, jnp.broadcast_to(logp, (pairs, 128)), 0.0), 1, keepdims=True) / slots
+    joint[...] = jnp.zeros_like(joint)
+    joint[0:pairs, :] = jnp.broadcast_to(reader, (pairs, 128))
+    joint_in[doc] = joint[...]
+    net.group("joint", [(joint, joint_in.at[doc], p) for p in doc_peers], lambda n: joint_in.at[pl.ds(0, n)])
+    shares = jnp.concatenate([f / whole for f in factors] + [rest / whole] + [jnp.zeros_like(peak)] * (15 - nb), 0).T
+
+    pl.loop(ff // chunk // 2, ff // chunk)(feed)
+    hat, _ = normed(acc[...])
+    block_out[...] = (hat * gain2 + shift2).astype(BF16)
+    net.collect("all tokens")
+    x4t[...] = x4[...].reshape(nd * rows, width).T
+
+    net.collect("hint")
     full_query = hints_in[0, 0:pairs, :]
     for j in range(1, nd):
         full_query += hints_in[j, 0:pairs, :]
     docs = [hints_in[j, 8 : 8 + pairs, :] for j in range(nd)]
     score = [jnp.broadcast_to(jnp.sum(full_query * d, 1, keepdims=True), (pairs, 128)) for d in docs]
-    for copy in joint_copies:
-        copy.wait_recv()
+    net.collect("joint")
     both = [s + joint_in[j, 0:pairs, :] for j, s in enumerate(score)]
 
     def soft(vals):
@@ -786,138 +932,175 @@
     for j in range(1, nd):
         mine = jnp.where(doc == j, w_joint[j], mine)
     row_weight = jnp.broadcast_to(mine.reshape(pairs, 1, 128), (pairs, slots, 128)).reshape(n_pick, 128)[:, 0:1]
+
+    net.collect("left")
+
+    def turn(route, lanes):
+        def go():
+            at[route][0:lanes, :] = a1[route][:, :, 0:lanes].reshape(8 * n_pick, lanes).T
+
+        return go
+
+    for route in range(2):
+        pl.when(core == 0)(turn(route, lanes0[route]))
+        pl.when(core == 1)(turn(route, lanes1[route]))
+
+    net.collect("back")
+    row_grad = jnp.zeros((n_pick, width), F32)
+    for j in range(nb):
+        row_grad += shares[0:n_pick, j : j + 1] * urecv[j].astype(F32)
+    net.collect("target")
+    at_target = target_rows[...].astype(F32).reshape(n_pick, width)
+    row_grad -= shares[0:n_pick, nb : nb + 1] * at_target
     final_grad = row_grad * (row_weight / slots)
 
-    g1_at, g2_at = net.take(8), net.take(8)
-    g1_send, g2_send = net.take(8), net.take(8)
-    half_w, half_f = width // 2, ff // 2
-
-    def send_right(src, cols, dst, to_core, send_at, recv_at):
-        for k, (dx, dz) in enumerate(sides):
-            peer, tx, _ = side_peer(dx, dz, to_core)
-            part = src.at[:, pl.ds(pl.multiple_of(tx * cols, 128), cols)]
-            land = dst.at[slot, :, pl.ds(0, cols)]
-            args = (part, land, peer, send_at + 2 * k + to_core, recv_at + 2 * k + core)
-            if k:
-                net.put(*args)
-            else:
-                net.put_if(core == 1 - to_core, *args)
-
-                def keep():
-                    dst[slot, :, 0:cols] = src[:, pl.ds(pl.multiple_of(x * cols, 128), cols)]
-
-                pl.when(core == to_core)(keep)
-
-    def wait_right(src, cols, dst, recv_at):
-        part = src.at[:, pl.ds(0, cols)]
-        land = dst.at[slot, :, pl.ds(0, cols)]
-        for k in range(4):
-            for from_core in range(2):
-                i = recv_at + 2 * k + from_core
-                if k:
-                    net.copy(part, land, twin, i, i).wait_recv()
-        i = recv_at + 1 - core
-        net.copy(part, land, twin, i, i).wait_recv()
+    def send_right(due, src, every, first, cols, dst, to_core, route):
+        def part(tx):
+            return pl.ds(pl.multiple_of(tx * every + first, 128), cols)
+
+        fan(due, lambda tx, tz: src.at[:, part(tx)], dst, cols, to_core, [0, 1], route)
+
+        def keep():
+            dst[slots_of[route], :, 0:cols] = src[:, part(x)]
+
+        pl.when(core == to_core)(keep)
 
     vecs[...] = jnp.zeros_like(vecs)
-    sum_grad = norm_back(final_grad, hat2, rstd2, gain2[...])
+    sum_grad = norm_back(final_grad, hat2, rstd2, gain2)
     vecs[6:7, :] = jnp.sum(final_grad * hat2, 0, keepdims=True)
     vecs[7:8, :] = jnp.sum(final_grad, 0, keepdims=True)
     vecs[5:6, :] = jnp.sum(sum_grad, 0, keepdims=True)
     second_low = sum_grad.astype(BF16)
     second_b[...] = second_low
-    send_right(second_b, half_w, g1, 0, g1_send, g1_at)
+    for route in range(2):
+        send_right(("g1", route), second_b, half_w, 0, half_w, g1[route], 0, route)
     inner_grad = mm_nt(second_low, wdown[...]) * gelu_slope(inner_p)
     inner_low = inner_grad.astype(BF16)
     inner_b[...] = inner_low
-    send_right(inner_b, half_f, g1, 1, g1_send, g1_at)
+    for route in range(2):
+        first, cols = firsts[route] * half_w, counts[route] * half_w
+        send_right(("g1", route), inner_b, half_f, first, cols, g1[route], 1, route)
     up_bias_grad = jnp.sum(inner_grad, 0, keepdims=True)
     for i in range(ff // width):
         vecs[8 + i : 9 + i, :] = up_bias_grad[:, i * width : (i + 1) * width]
     first_grad = sum_grad + mm_nt(inner_low, wup[...])
-    resid_grad = norm_back(first_grad, hat1, rstd1, gain1[...])
+    resid_grad = norm_back(first_grad, hat1, rstd1, gain1)
     resid_low = resid_grad.astype(BF16)
     rest_b[0] = resid_low
-    send_right(rest_b.at[0], half_w, g2, 0, g2_send, g2_at)
+    send_right("g2", rest_b.at[0], half_w, 0, half_w, g2, 0, 0)
     vecs[3:4, :] = jnp.sum(first_grad * hat1, 0, keepdims=True)
     vecs[4:5, :] = jnp.sum(first_grad, 0, keepdims=True)
     vecs[2:3, :] = jnp.sum(resid_grad, 0, keepdims=True)
-    mixed_grad = expand(mm_nt(resid_low, wout[...]).astype(BF16))
+    mixed_grad_p = mm_nt(resid_low, wout[...]).astype(BF16)
+    halves(qm_send.at[1], mixed_grad_p)
+    half_heads("heads", qm_send.at[1], qm, 1)
+    mixed_grad = expand(mixed_grad_p)
     prob_grad = mm_nt(mixed_grad, vb[...])
-    value_grad = mm_tn(probs_low[...], mixed_grad)
     p = probs[...]
     score_low = (p * (prob_grad - jnp.sum(prob_grad * p, -1, keepdims=True)) * scale).astype(BF16)
-    key_grad = mm_tn(score_low, qexp[...])
-    kvb[0] = key_grad.astype(BF16)
-    kvb[1] = value_grad.astype(BF16)
-    kv_at = net.take()
-    kv_copy = net.put(kvb.at[1 - core], kv2.at[pl.ds(rows, rows)], twin, kv_at, kv_at)
-    kv2[0:rows, :] = kvb[core]
+    sp_send[0] = score_low.reshape(2, tall_half, rows)
+    half_heads("heads", sp_send.at[0], sp, 0)
     query_grad_p = fold(mm(score_low, kb[...]))
     rest_b[1] = query_grad_p.astype(BF16)
-    send_right(rest_b.at[1], half_w, g2, 1, g2_send, g2_at)
+    send_right("g2", rest_b.at[1], half_w, 0, half_w, g2, 1, 0)
     vecs[0:1, :] = jnp.sum(query_grad_p, 0, keepdims=True)
+    value_grad = mm_tn(probs_low[...], mixed_grad)
+    kvb[1] = value_grad.astype(BF16)
     vecs[1:2, :] = jnp.sum(value_grad, 0, keepdims=True)
 
-    runs = []
-    bufs = list(trip_bufs)
+    sems = [[net.take() for _ in t.steps] for t in trips]
+    groups, left_over = [], list(trip_bufs)
     for t in trips:
         k = len(t.buffers())
-        runs.append(TripRun(t, bufs[:k], net, spot))
-        bufs = bufs[k:]
-    runs[8].bufs[0][...] = vecs[...].astype(BF16)
-    runs[8].start(0)
-    wait_left()
-    at[0 : 2 * width, :] = a1[...].reshape(8 * n_pick, 2 * width).T
-    at[2 * width : 3 * width, :] = a2[...].reshape(8 * n_pick, width).T
-    quads = [(z1, y) for z1 in range(2) for y in range(2)]
-
-    def block(i, offsets, g, col):
-        left = jnp.concatenate([at[pl.ds(pl.multiple_of(o, 32), share), :] for o in offsets], 0)
-        right = g[:, :, pl.ds(col, half_w)].reshape(8 * n_pick, half_w)
-        out = mm(left, right).astype(BF16)
-        for n, (z1, y) in enumerate(quads):
-            runs[i].bufs[0][z1, y] = out[n * share : (n + 1) * share]
-        runs[i].start(0)
-
-    pl.when(core == 0)(lambda: wait_right(second_b, half_w, g1, g1_at))
-    pl.when(core == 1)(lambda: wait_right(inner_b, half_f, g1, g1_at))
-    for i in range(4):
-        offsets = [
-            (1 - core) * ((2 * z1 + y) * 4 * share + i * share) + core * (4 * z1 + 2 * z0 + y) * share
-            for z1, y in quads
-        ]
-        block(i, offsets, g1, pl.multiple_of(core * i * half_w, 128))
-
-    kv_copy.wait_recv()
-    for j in range(3):
-        right = jnp.concatenate([kv2[:, s * half_w + 128 * j : s * half_w + 128 * (j + 1)] for s in range(2)], 1)
-        out = mm(x2t[...], right).astype(BF16)
-        for s in range(2):
+        groups.append(left_over[:k])
+        left_over = left_over[k:]
+
+    def tail(side, net):
+        runs = [TripRun(t, groups[n], sems[n], net, spot) for n, t in enumerate(trips)]
+
+        def make_wide():
+            net.collect("heads")
+            half_tall = iota((tall_half, half_w), 0) // n_pick == iota((tall_half, half_w), 1) // HEAD_DIM
+            for d in range(nd):
+                tiled = jnp.concatenate([qm[d]] * (heads // 2), 0)
+                tiled = jnp.where(half_tall, tiled, jnp.zeros((), BF16))
+                kv4[d] = mm_tn(sp[d], tiled).astype(BF16)
+            right = kv4[...].reshape(nd * rows, half_w)
             for b in range(nb):
-                runs[5 + j].bufs[0][s, b // 4, b // 2 % 2, b % 2] = out[
-                    b * share : (b + 1) * share, 128 * s : 128 * (s + 1)
-                ]
-        runs[5 + j].start(0)
-    wait_right(rest_b.at[0], half_w, g2, g2_at)
-    block(4, [2 * width - width * core + (4 * z1 + 2 * z0 + y) * share for z1, y in quads], g2, 0)
-
-    inward = mm_nt(kvb[0], wqkv[:, width : 2 * width]) + mm_nt(kvb[1], wqkv[:, 2 * width :])
-    at_rows = resid_grad + mm_nt(rest_b[1], wqkv[:, 0:width])
-    grad_in[...] = (inward + mm_exact(pick_f32, at_rows, TN)).astype(BF16)
-
-    ready = [0.0, 0.4, 0.8, 1.2, 5.0, 3.0, 3.5, 4.0, 0.0]
-    for i, step in exchange_order(trips, ready, link_table(8, 4)):
-        runs[i].finish(step)
-        if step + 1 < len(trips[i].steps):
-            runs[i].start(step + 1)
-        elif i < 5:
-            mats_out[i] = runs[i].final[...]
-        elif i < 8:
-            wide_out[i - 5] = runs[i].final[...]
-        else:
-            vec_out[...] = runs[i].final[...]
-    net.drain()
+                out = mm(x4t[b * share : (b + 1) * share, :], right).astype(BF16)
+                for n in range(3):
+                    runs[5 + n].bufs[0][b // 4, b // 2 % 2, b % 2] = out[:, 128 * n : 128 * (n + 1)]
+
+        def block(i, route, offsets, g, col):
+            left = jnp.concatenate([at[route][pl.ds(pl.multiple_of(o, 32), share), :] for o in offsets], 0)
+            right = g[:, :, pl.ds(col, half_w)].reshape(8 * n_pick, half_w)
+            out = mm(left, right).astype(BF16)
+            for n, (z1, other) in enumerate(quads):
+                runs[i].bufs[0][z1, other] = out[n * share : (n + 1) * share]
+
+        def make_blocks(route):
+            net.collect(("g1", route))
+            for i in range(counts[route]):
+                offsets = [((1 - core) * (n * counts[route] + i) + core * n) * share for n in range(4)]
+                block(firsts[route] + i, route, offsets, g1[route], pl.multiple_of(core * i * half_w, 128))
+
+        def make_last():
+            net.collect("g2")
+            first_row = (1 - core) * 4 * share * counts[0] + core * 4 * share
+            block(4, 0, [first_row + n * share for n in range(4)], g2, 0)
+
+        def make_inward():
+            kvb[0] = mm_tn(score_low, qexp[...]).astype(BF16)
+            inward = mm_nt(kvb[0], wqkv[:, width : 2 * width]) + mm_nt(kvb[1], wqkv[:, 2 * width :])
+            at_rows = resid_grad + mm_nt(rest_b[1], wqkv[:, 0:width])
+            grad_in[...] = (inward + mm_exact(pick_f32, at_rows, TN)).astype(BF16)
+
+        def make_sums():
+            runs[8].bufs[0][...] = vecs[...].astype(BF16)
+
+        along_y = list(range(ALONG_Z, 4))
+        along_z = list(range(ALONG_Z))
+        stages = (
+            [
+                (0.0, [8], make_sums),
+                (0.6, along_y, lambda: make_blocks(1)),
+                (1.2, along_z, lambda: make_blocks(0)),
+                (1.8, [4], make_last),
+                (5.0, [5, 6, 7], make_wide),
+                (9.0, [], make_inward),
+            ]
+            if side == 0
+            else [
+                (0.0, [8], make_sums),
+                (2.5, [5, 6, 7], make_wide),
+                (5.0, along_y, lambda: make_blocks(1)),
+                (5.6, along_z, lambda: make_blocks(0)),
+                (6.2, [4], make_last),
+                (10.0, [], make_inward),
+            ]
+        )
+        last = []
+        for what, i, step in trip_program(trips, [(t, made) for t, made, _ in stages]):
+            if what == "make":
+                stages[i][2]()
+            elif what == "start":
+                runs[i].start(step)
+            elif trips[i].steps[step][1] == ("doc", 0):
+                last.append((i, step))
+            else:
+                runs[i].finish(step)
+        for i, step in last:
+            runs[i].finish(step)
+            if i < 5:
+                mats_out[i] = runs[i].final[...]
+            elif i < 8:
+                wide_out[i - 5] = runs[i].final[...]
+            else:
+                vec_out[...] = runs[i].final[...]
+        net.drain()
+
+    for side in range(2):
+        pl.when(core == side)(partial(tail, side, net.branch()))
 
 
 def finish_kernel(block, grad, loss, gq, mats, wide, vec, *outs):
@@ -947,7 +1130,7 @@
     for i, o in enumerate((o_qb, o_vb, o_ob, o_g1, o_s1, o_db, o_g2, o_s2)):
         o[...] = got[i : i + 1, :]
     side = jnp.where(lax.rem(batch, 2) == 0, v[8:12, 0:half], v[8:12, half:])
-    o_ub[...] = jnp.sum(jnp.where(iota((4, half), 0) == batch // 2, side, 0.0), 0, keepdims=True)
+    o_ub[...] = jnp.sum(jnp.where(iota((4, half), 0) == batch // 2, side, 0.0), 0)
 
 
 def paired_local(*args):
@@ -965,6 +1148,8 @@
     share = width // nb
     heads = width // HEAD_DIM
     trips = layer_trips(share)
+    lanes_z, lanes_y = 4 * share * (ALONG_Z + 1), 4 * share * (4 - ALONG_Z)
+    n_sems = sum(len(t.steps) for t in trips) + 28
     vm, hbm = pl.BlockSpec(memory_space=pltpu.VMEM), pl.BlockSpec(memory_space=pl.ANY)
 
     def v(shape, dtype=BF16):
@@ -975,16 +1160,21 @@
         v(qkv_weight.shape), v(out_weight.shape), v(up_weight.shape), v(down_weight.shape), v(vocab.shape),
         v((rows, width)), v((rows, width)), v((rows, width)), v((rows, width)),
         v((rows, width), F32), v((rows, width)), v((rows, width), F32),
-        v((2 * rows, width)), v((width, 2 * rows)), v((2, rows, width)), v((2 * rows, width)),
-        v((nb, n_pick, width)), v((nb, n_pick, width)), v((nb, n_pick, width)), v((nb, n_pick, width)),
-        v((nb, n_pick, width)), v((nb, n_pick, 128), F32), v((nb, n_pick, 128), F32), v((nb * n_pick, entries), F32),
+        v((nd, rows, width)), v((width, nd * rows)), v((2, rows, width)), v((nd, rows, width // 2)),
+        v((nd, heads * n_pick // 2, rows)), v((2, 2, heads * n_pick // 2, rows)),
+        v((nd, n_pick, width // 2)), v((2, 2, n_pick, width // 2)),
+        v((nb, n_pick, width)), v((nb, nd, n_pick // nd, width)), v((nb, n_pick // nd, width)),
+        v((nd, n_pick // nd, width)), v((nb, n_pick, width)),
+        v((nb, n_pick, width)), v((nb, 8, 128), F32), v((nb, 8, 128), F32), v((nb * n_pick, entries), F32),
         v((heads * n_pick, width)), v((heads * n_pick, rows), F32), v((heads * n_pick, rows)),
         v((16, 128), F32), v((nd, 16, 128), F32), v((8, 128), F32), v((nd, 8, 128), F32),
-        v((3, n_pick, 2 * width)), v((n_pick, width)), v((8, n_pick, 2 * width)), v((8, n_pick, width)),
-        v((3 * width, 8 * n_pick)), v((n_pick, width)), v((n_pick, ff)), v((2, n_pick, width)),
-        v((8, n_pick, ff // 2)), v((8, n_pick, width // 2)),
-        v((16, width), F32),
-        dma((6,)), dma((256,)), dma((256,)),
+        v((2, n_pick, lanes_z)), v((2, n_pick, lanes_y)), v((2, n_pick, width)), v((2, n_pick, width // 2)),
+        v((8, n_pick, lanes_z)), v((8, n_pick, max(lanes_y, width // 2))), v((lanes_z, 8 * n_pick)),
+        v((max(lanes_y, width // 2), 8 * n_pick)),
+        v((n_pick, width)), v((n_pick, ff)), v((2, n_pick, width)),
+        v((8, n_pick, ALONG_Z * width // 2)), v((8, n_pick, (4 - ALONG_Z) * width // 2)), v((8, n_pick, width // 2)),
+        v((16, width), F32), v((1, ff), F32),
+        dma((6,)), dma((n_sems,)), dma((n_sems,)),
     ]
     for t in trips:
         scratch += [v(shape) for shape in t.buffers()]
@@ -1016,7 +1206,7 @@
         target_ids,
         query_emb.reshape(pairs, -1),
         doc_emb.reshape(pairs, -1),
-        *[b.reshape(1, -1) for b in biases],
+        *biases,
         qkv_weight,
         out_weight,
         up_weight,
@@ -1029,7 +1219,7 @@
         out_shape=[
             sds((rows, width), BF16), sds((1, pairs), F32), sds((rows, width), BF16), sds(gq.shape, F32),
             sds((share, 3 * width), F32), small, small, sds((share, width), F32), small, small, small,
-            sds((share, ff), F32), sds((1, ff // nb), F32), sds((ff // nb, width), F32), small, small, small,
+            sds((share, ff), F32), sds((ff // nb,), F32), sds((ff // nb, width), F32), small, small, small,
         ],
         in_specs=[vm] * 7,
         out_specs=[vm] * 17,
@@ -1038,7 +1228,7 @@
     )(block, grad, loss, gq, mats, wide, vec)
     shapes = [hidden_in.shape, (1, pairs), hidden_in.shape, query_emb.shape]
     fixed = [o.reshape(s) for o, s in zip(outs[:4], shapes)]
-    return tuple(fixed + [o.reshape(-1) if o.shape[0] == 1 else o for o in outs[4:]])
+    return tuple(fixed + [o.reshape(-1) if o.shape == (1, share) else o for o in outs[4:]])
 
 
 def combined_all(x, axis, combine):

time: 117 us -> 86.6 us (0.74)
  Pallas kernels: 104 us -> 85.6 us
  local copies, waits for them, and re-layouts: 10.2 us -> 0 us
  other arithmetic: 1.27 us -> 0 us
    pallas_call x1, Pallas kernels: 100 us -> 81.5 us  [paired_local(): first(hidden_in.reshape(rows, width), segments.reshape(1, rows), mask_pos...]
    reshape x8 -> x0, local copies, waits for them, and re-layouts: 10.2 us -> none  [paired_local(): b.reshape(1, -1)]
    pallas_call x1 -> x0, other arithmetic: 1.27 us -> none  [paired_local(): pl.pallas_call(finish_kernel, out_shape=[sds((rows, width), BF16), sds((1...]
where the time goes in v2:
time: 86.6 us; the launch traced here: 86.4 us
  Pallas kernels  85.6 us (99%)
    pallas_call x1, Pallas kernels, paired_local(): first(hidden_in.reshape(rows, width), segments.reshape(1, rows), mask_pos...  81.5 us
    pallas_call x1, Pallas kernels, paired_local(): pl.pallas_call(finish_kernel, out_shape=[sds((rows, width), BF16), sds((1...  4.13 us

profile of v2, /device:TPU:0, one launch (start us, length us, event | category | flops | bytes accessed | tf_op | source)
XLA Modules:
  0.0 86.4 jit_solution(2365012701316877212)
XLA Ops:
  0.7 81.5 %layer.1 = (bf16[288,768]{1,0:T(8,128)(2,1)}, f32[1,128]{1,0:T(1,128)}, bf16[288,768]{1,0:T(8,128)(2,1)}, f32[4,32]{1,0:T(4,128)}, bf16[5,2,2,96,384]{4,3,2,1,0:...) custom-call(bf16[288,768]{1,0:T(8,128)(2,1)} %bitcast.16, s32[1,288]{1,0:T(1,128)} %bitcast.20, ...), custom_call_target="tpu_custom_call" | custom-call | tf_op jit(solution)/shard_map/layer/pallas_call | solution.py:1202
  82.1 4.1 %finish.1 = (bf16[288,768]{1,0:T(8,128)(2,1)}, f32[1,4]{1,0:T(1,128)}, bf16[288,768]{1,0:T(8,128)(2,1)}, f32[4,32]{1,0:T(4,128)}, f32[96,2304]{1,0:T(8,128)}, /*...) custom-call(bf16[288,768]{1,0:T(8,128)(2,1)} %get-tuple-element.41.b, ...), custom_call_target="tpu_custom_call" | custom-call | tf_op jit(solution)/shard_map/finish/pallas_call | solution.py:1217

commit v3 on v2

--- a/solution.py
+++ b/solution.py
@@ -433,7 +433,7 @@
         shapes = [(2,) * len(self.lead) + self.tile]
         shapes += [(2,) * (len(self.lead) - i - 1) + self.tile for i in range(len(self.halve))]
         shapes += [self.tile] * len(self.both)
-        return shapes + [((2, 2) if self.end else ()) + self.tile]
+        return shapes + [((4,) if self.end else ()) + self.tile]
 
     def bytes(self, i):
         kind, key = self.steps[i]
@@ -456,7 +456,7 @@
         return tuple(fixed.get(key, slice(None)) for key in self.t.lead)
 
     def place(self):
-        return (self.spot.mine(("doc", 0)), self.spot.mine(("doc", 1))) if self.t.end else ()
+        return (2 * self.spot.mine(("doc", 0)) + self.spot.mine(("doc", 1)),) if self.t.end else ()
 
     def start(self, step):
         kind, key = self.t.steps[step]
@@ -465,12 +465,10 @@
             sem = self.at_step[step]
             for peer in self.spot.others():
                 self.net.put(mine, mine, peer, sem)
-            pair, one = self.final.at[0], self.final.at[0, 0]
-            peer = self.spot.peer(("doc", 0))
-            for view in (pair, one):
-                copy = self.net.copy(view, view, peer, sem)
-                self.net.expect(sem, copy.wait_recv)
-                self.net.open.append(copy.wait_send)
+            view = self.final.at[pl.ds(0, 3)]
+            copy = self.net.copy(view, view, self.spot.peer(("doc", 0)), sem)
+            self.net.expect(sem, copy.wait_recv)
+            self.net.open.append(copy.wait_send)
             return
         if kind == "halve":
             src = self.bufs[0].at[self.at({**self.live, key: 1 - self.spot.mine(key)})]
@@ -480,7 +478,7 @@
         elif kind == "spread":
             src = dst = self.final.at[self.place()]
         else:
-            src = dst = self.final.at[self.spot.mine(key)]
+            src = dst = self.final.at[pl.ds(2 * self.spot.mine(key), 2)]
         at = self.at_step[step]
         copy = self.net.copy(src, dst, self.spot.peer(key), at)
         copy.start()
@@ -516,7 +514,7 @@
     block += [Trip((share, 384), [z1, z0], [z0, z1], [], "two") for _ in range(4 - ALONG_Z)]
     block += [Trip((share, 384), [z1, y], [y, z1], [], "two")]
     orders = [[y, z0, z1], [y, z0, z1], [y, z0, z1]]
-    wide = [Trip((share, 128), [z1, z0, y], order, [], "two") for order in orders]
+    wide = [Trip((share, 128), [z1, z0, y], order, [], "three") for order in orders]
     small = Trip((16, 768), [], [], [y, z0, z1, x, ("doc", 0)], "")
     return block + wide + [small]
 
@@ -529,7 +527,7 @@
     ("doc", 0): [("twin", 0.2)],
     None: [("x", 2.0)],
 }
-IN_FLIGHT = 2
+IN_FLIGHT = 3
 LINK_RATE = 91e3
 
 
@@ -662,8 +660,18 @@
     barrier = pltpu.get_barrier_semaphore()
     for peer in everyone:
         pl.semaphore_signal(barrier, inc=1, device_id=peer, device_id_type=MESH)
+
+    place_col = column_of(places[...])
+    pick_bool = iota((n_pick, rows), 1) == place_col
+    pick = pick_bool.astype(BF16)
+    pick_f32 = pick_bool.astype(F32)
+    tokens = hidden[...]
+    loads[0].wait()
+    kb[...] = mm(tokens, wqkv[:, width : 2 * width]).astype(BF16)
+    vb[...] = (mm(tokens, wqkv[:, 2 * width :]) + bias_v).astype(BF16)
+    tokens_p = mm(pick, tokens).astype(BF16)
+
     pl.semaphore_wait(barrier, len(everyone))
-
     own_part = query.shape[1]
     spread_lanes = (iota((own_part, own_part * nd), 0) + own_part * doc == iota((own_part, own_part * nd), 1)).astype(F32)
     hints[0:pairs, :] = mm_exact(query[...], spread_lanes)
@@ -675,16 +683,6 @@
     net.group("tokens", [(hidden, x4.at[doc], beside)], lambda n: x4.at[pl.ds(0, n)])
     net.group("all tokens", [(hidden, x4.at[doc], twin)], lambda n: x4.at[pl.ds(0, n)])
     x4[doc] = hidden[...]
-
-    place_col = column_of(places[...])
-    pick_bool = iota((n_pick, rows), 1) == place_col
-    pick = pick_bool.astype(BF16)
-    pick_f32 = pick_bool.astype(F32)
-    tokens = hidden[...]
-    loads[0].wait()
-    kb[...] = mm(tokens, wqkv[:, width : 2 * width]).astype(BF16)
-    vb[...] = (mm(tokens, wqkv[:, 2 * width :]) + bias_v).astype(BF16)
-    tokens_p = mm(pick, tokens).astype(BF16)
 
     loads[1].wait()
     entries = wvoc.shape[0]
@@ -1066,8 +1064,8 @@
                 (0.6, along_y, lambda: make_blocks(1)),
                 (1.2, along_z, lambda: make_blocks(0)),
                 (1.8, [4], make_last),
-                (5.0, [5, 6, 7], make_wide),
-                (9.0, [], make_inward),
+                (8.0, [5, 6, 7], make_wide),
+                (12.0, [], make_inward),
             ]
             if side == 0
             else [
@@ -1085,16 +1083,16 @@
                 stages[i][2]()
             elif what == "start":
                 runs[i].start(step)
-            elif trips[i].steps[step][1] == ("doc", 0):
+            elif trips[i].steps[step][1] in (("doc", 0), None):
                 last.append((i, step))
             else:
                 runs[i].finish(step)
         for i, step in last:
             runs[i].finish(step)
             if i < 5:
-                mats_out[i] = runs[i].final[...]
+                mats_out[i] = runs[i].final[...].reshape(mats_out.shape[1:])
             elif i < 8:
-                wide_out[i - 5] = runs[i].final[...]
+                wide_out[i - 5] = runs[i].final[...].reshape(wide_out.shape[1:])
             else:
                 vec_out[...] = runs[i].final[...]
         net.drain()

time: 86.6 us -> 80.9 us (0.934)
  Pallas kernels: 85.6 us -> 79.9 us
    pallas_call x1, Pallas kernels: 81.5 us -> 75.8 us  [paired_local(): first(hidden_in.reshape(rows, width), segments.reshape(1, rows), mask_pos...]
where the time goes in v3:
time: 80.9 us; the launch traced here: 80.7 us
  Pallas kernels  79.9 us (99%)
  between operations  0.85 us (1%)
    pallas_call x1, Pallas kernels, paired_local(): first(hidden_in.reshape(rows, width), segments.reshape(1, rows), mask_pos...  75.8 us
    pallas_call x1, Pallas kernels, paired_local(): pl.pallas_call(finish_kernel, out_shape=[sds((rows, width), BF16), sds((1...  4.13 us

profile of v3, /device:TPU:0, one launch (start us, length us, event | category | flops | bytes accessed | tf_op | source)
XLA Modules:
  0.0 80.7 jit_solution(12211583833086083856)
XLA Ops:
  0.7 75.8 %layer.1 = (bf16[288,768]{1,0:T(8,128)(2,1)}, f32[1,128]{1,0:T(1,128)}, bf16[288,768]{1,0:T(8,128)(2,1)}, f32[4,32]{1,0:T(4,128)}, bf16[5,2,2,96,384]{4,3,2,1,0:...) custom-call(bf16[288,768]{1,0:T(8,128)(2,1)} %bitcast.16, s32[1,288]{1,0:T(1,128)} %bitcast.20, ...), custom_call_target="tpu_custom_call" | custom-call | tf_op jit(solution)/shard_map/layer/pallas_call | solution.py:1200
  76.4 4.1 %finish.1 = (bf16[288,768]{1,0:T(8,128)(2,1)}, f32[1,4]{1,0:T(1,128)}, bf16[288,768]{1,0:T(8,128)(2,1)}, f32[4,32]{1,0:T(4,128)}, f32[96,2304]{1,0:T(8,128)}, /*...) custom-call(bf16[288,768]{1,0:T(8,128)(2,1)} %get-tuple-element.41.b, ...), custom_call_target="tpu_custom_call" | custom-call | tf_op jit(solution)/shard_map/finish/pallas_call | solution.py:1215

commit v4 on v3

--- a/solution.py
+++ b/solution.py
@@ -528,7 +528,7 @@
     None: [("x", 2.0)],
 }
 IN_FLIGHT = 3
-LINK_RATE = 91e3
+LINK_RATE = 100e3
 
 
 def trip_program(trips, stages):
@@ -581,7 +581,7 @@
         hints, hints_in, joint, joint_in,
         left0, left0_y, left1, left1_y, a1, a1_y, at, at_y, second_b, inner_b, rest_b, g1, g1_y, g2,
         vecs, up_bias_s,
-        load_sem, send, recv, *trip_bufs,
+        block_v, grad_v, load_sem, store_sem, send, recv, *trip_bufs,
     ) = refs
     bias_q, bias_v, bias_o, gain1, shift1, bias_up, bias_down, gain2, shift2 = (
         b[...].reshape(1, -1) for b in (bias_q, bias_v, bias_o, gain1, shift1, bias_up, bias_down, gain2, shift2)
@@ -895,7 +895,9 @@
 
     pl.loop(ff // chunk // 2, ff // chunk)(feed)
     hat, _ = normed(acc[...])
-    block_out[...] = (hat * gain2 + shift2).astype(BF16)
+    block_v[...] = (hat * gain2 + shift2).astype(BF16)
+    block_store = pltpu.make_async_copy(block_v, block_out, store_sem.at[8])
+    block_store.start()
     net.collect("all tokens")
     x4t[...] = x4[...].reshape(nd * rows, width).T
 
@@ -1015,6 +1017,12 @@
 
     def tail(side, net):
         runs = [TripRun(t, groups[n], sems[n], net, spot) for n, t in enumerate(trips)]
+        stores = []
+
+        def store(src, dst, n):
+            copy = pltpu.make_async_copy(src, dst, store_sem.at[n])
+            copy.start()
+            stores.append(copy)
 
         def make_wide():
             net.collect("heads")
@@ -1051,7 +1059,8 @@
             kvb[0] = mm_tn(score_low, qexp[...]).astype(BF16)
             inward = mm_nt(kvb[0], wqkv[:, width : 2 * width]) + mm_nt(kvb[1], wqkv[:, 2 * width :])
             at_rows = resid_grad + mm_nt(rest_b[1], wqkv[:, 0:width])
-            grad_in[...] = (inward + mm_exact(pick_f32, at_rows, TN)).astype(BF16)
+            grad_v[...] = (inward + mm_exact(pick_f32, at_rows, TN)).astype(BF16)
+            store(grad_v, grad_in, 9)
 
         def make_sums():
             runs[8].bufs[0][...] = vecs[...].astype(BF16)
@@ -1090,15 +1099,18 @@
         for i, step in last:
             runs[i].finish(step)
             if i < 5:
-                mats_out[i] = runs[i].final[...].reshape(mats_out.shape[1:])
+                store(runs[i].final, mats_out.at[i], i)
             elif i < 8:
-                wide_out[i - 5] = runs[i].final[...].reshape(wide_out.shape[1:])
+                store(runs[i].final, wide_out.at[i - 5], i)
             else:
                 vec_out[...] = runs[i].final[...]
+        for copy in stores:
+            copy.wait()
         net.drain()
 
     for side in range(2):
         pl.when(core == side)(partial(tail, side, net.branch()))
+    block_store.wait()
 
 
 def finish_kernel(block, grad, loss, gq, mats, wide, vec, *outs):
@@ -1113,15 +1125,15 @@
     o_gq[...] = gq[...]
     for s in range(2):
         cols = slice(s * half, (s + 1) * half)
-        o_out[:, cols] = mats[4, 0, s].astype(F32)
-        o_qkv[:, cols] = mats[4, 1, s].astype(F32)
+        o_out[:, cols] = mats[4, s].astype(F32)
+        o_qkv[:, cols] = mats[4, 2 + s].astype(F32)
         for i in range(4):
-            o_down[i * share : (i + 1) * share, cols] = mats[i, 0, s].astype(F32)
-            o_up[:, (4 * s + i) * half : (4 * s + i + 1) * half] = mats[i, 1, s].astype(F32)
+            o_down[i * share : (i + 1) * share, cols] = mats[i, s].astype(F32)
+            o_up[:, (4 * s + i) * half : (4 * s + i + 1) * half] = mats[i, 2 + s].astype(F32)
         for c in range(2):
             for j in range(3):
                 start = (1 + c) * width + s * half + 128 * j
-                o_qkv[:, start : start + 128] = wide[j, c, s].astype(F32)
+                o_qkv[:, start : start + 128] = wide[j, 2 * c + s].astype(F32)
     v = vec[...].astype(F32)
     take = (iota((width, share), 0) == iota((width, share), 1) + batch * share).astype(F32)
     got = mm_exact(v, take)
@@ -1172,7 +1184,7 @@
         v((n_pick, width)), v((n_pick, ff)), v((2, n_pick, width)),
         v((8, n_pick, ALONG_Z * width // 2)), v((8, n_pick, (4 - ALONG_Z) * width // 2)), v((8, n_pick, width // 2)),
         v((16, width), F32), v((1, ff), F32),
-        dma((6,)), dma((n_sems,)), dma((n_sems,)),
+        v((rows, width)), v((rows, width)), dma((6,)), dma((10,)), dma((n_sems,)), dma((n_sems,)),
     ]
     for t in trips:
         scratch += [v(shape) for shape in t.buffers()]
@@ -1184,12 +1196,12 @@
             sds((1, 128), F32),
             sds((rows, width), BF16),
             sds((pairs, query_emb.shape[2]), F32),
-            sds((5, 2, 2, share, 384), BF16),
-            sds((3, 2, 2, share, 128), BF16),
+            sds((5, 4, share, 384), BF16),
+            sds((3, 4, share, 128), BF16),
             sds((16, width), BF16),
         ],
         in_specs=[vm] * 15 + [hbm] * 5,
-        out_specs=[vm] * 7,
+        out_specs=[hbm, vm, hbm, vm, hbm, hbm, vm],
         scratch_shapes=scratch,
         compiler_params=pltpu.CompilerParams(
             collective_id=0, has_side_effects=True, vmem_limit_bytes=VMEM_BYTES

time: 80.9 us -> 80.1 us (level)
  no operation moved by 1% of the time
where the time goes in v4:
time: 80.1 us; the launch traced here: 79.9 us
  Pallas kernels  79.1 us (99%)
  between operations  0.85 us (1%)
    pallas_call x1, Pallas kernels, paired_local(): first(hidden_in.reshape(rows, width), segments.reshape(1, rows), mask_pos...  75 us
    pallas_call x1, Pallas kernels, paired_local(): pl.pallas_call(finish_kernel, out_shape=[sds((rows, width), BF16), sds((1...  4.13 us

profile of v4, /device:TPU:0, one launch (start us, length us, event | category | flops | bytes accessed | tf_op | source)
XLA Modules:
  0.0 79.9 jit_solution(6356819997290262090)
XLA Ops:
  0.7 75.0 %layer.1 = (bf16[288,768]{1,0:T(8,128)(2,1)}, f32[1,128]{1,0:T(1,128)}, bf16[288,768]{1,0:T(8,128)(2,1)}, f32[4,32]{1,0:T(4,128)}, bf16[5,4,96,384]{3,2,1,0:T(8,...) custom-call(bf16[288,768]{1,0:T(8,128)(2,1)} %bitcast.16, s32[1,288]{1,0:T(1,128)} %bitcast.20, ...), custom_call_target="tpu_custom_call" | custom-call | tf_op jit(solution)/shard_map/layer/pallas_call | solution.py:1212
  75.6 4.1 %finish.1 = (bf16[288,768]{1,0:T(8,128)(2,1)}, f32[1,4]{1,0:T(1,128)}, bf16[288,768]{1,0:T(8,128)(2,1)}, f32[4,32]{1,0:T(4,128)}, f32[96,2304]{1,0:T(8,128)}, /*...) custom-call(bf16[288,768]{1,0:T(8,128)(2,1)} %get-tuple-element.41.b, ...), custom_call_target="tpu_custom_call" | custom-call | tf_op jit(solution)/shard_map/finish/pallas_call | solution.py:1227

commit v5 on v4

--- a/solution.py
+++ b/solution.py
@@ -386,6 +386,11 @@
         self.recvs += 1
         return self.sends - 1, self.recvs - 1
 
+    def take_chain(self, n):
+        self.sends += 1
+        self.recvs += n
+        return [(self.sends - 1, self.recvs - n + i) for i in range(n)]
+
     def copy(self, src, dst, peer, at):
         return pltpu.make_async_remote_copy(
             src_ref=src,
@@ -468,7 +473,7 @@
             view = self.final.at[pl.ds(0, 3)]
             copy = self.net.copy(view, view, self.spot.peer(("doc", 0)), sem)
             self.net.expect(sem, copy.wait_recv)
-            self.net.open.append(copy.wait_send)
+            self.net.expect(sem, copy.wait_send)
             return
         if kind == "halve":
             src = self.bufs[0].at[self.at({**self.live, key: 1 - self.spot.mine(key)})]
@@ -483,10 +488,7 @@
         copy = self.net.copy(src, dst, self.spot.peer(key), at)
         copy.start()
         self.net.expect(at, copy.wait_recv)
-        if kind == "both":
-            self.net.expect(at, copy.wait_send)
-        else:
-            self.net.open.append(copy.wait_send)
+        self.net.expect(at, copy.wait_send)
 
     def finish(self, step):
         kind, key = self.t.steps[step]
@@ -528,7 +530,7 @@
     None: [("x", 2.0)],
 }
 IN_FLIGHT = 3
-LINK_RATE = 100e3
+LINK_RATE = 115e3
 
 
 def trip_program(trips, stages):
@@ -1008,7 +1010,7 @@
     kvb[1] = value_grad.astype(BF16)
     vecs[1:2, :] = jnp.sum(value_grad, 0, keepdims=True)
 
-    sems = [[net.take() for _ in t.steps] for t in trips]
+    sems = [net.take_chain(len(t.steps)) for t in trips]
     groups, left_over = [], list(trip_bufs)
     for t in trips:
         k = len(t.buffers())
@@ -1160,6 +1162,7 @@
     trips = layer_trips(share)
     lanes_z, lanes_y = 4 * share * (ALONG_Z + 1), 4 * share * (4 - ALONG_Z)
     n_sems = sum(len(t.steps) for t in trips) + 28
+    n_sends = len(trips) + 28
     vm, hbm = pl.BlockSpec(memory_space=pltpu.VMEM), pl.BlockSpec(memory_space=pl.ANY)
 
     def v(shape, dtype=BF16):
@@ -1184,7 +1187,7 @@
         v((n_pick, width)), v((n_pick, ff)), v((2, n_pick, width)),
         v((8, n_pick, ALONG_Z * width // 2)), v((8, n_pick, (4 - ALONG_Z) * width // 2)), v((8, n_pick, width // 2)),
         v((16, width), F32), v((1, ff), F32),
-        v((rows, width)), v((rows, width)), dma((6,)), dma((10,)), dma((n_sems,)), dma((n_sems,)),
+        v((rows, width)), v((rows, width)), dma((6,)), dma((10,)), dma((n_sends,)), dma((n_sems,)),
     ]
     for t in trips:
         scratch += [v(shape) for shape in t.buffers()]

time: 80.1 us -> 80 us (level)
  no operation moved by 1% of the time
where the time goes in v5:
time: 80 us; the launch traced here: 79.8 us
  Pallas kernels  78.9 us (99%)
  between operations  0.85 us (1%)
    pallas_call x1, Pallas kernels, paired_local(): first(hidden_in.reshape(rows, width), segments.reshape(1, rows), mask_pos...  74.8 us
    pallas_call x1, Pallas kernels, paired_local(): pl.pallas_call(finish_kernel, out_shape=[sds((rows, width), BF16), sds((1...  4.13 us

profile of v5, /device:TPU:0, one launch (start us, length us, event | category | flops | bytes accessed | tf_op | source)
XLA Modules:
  0.0 79.8 jit_solution(13903675254850316982)
XLA Ops:
  0.7 74.8 %layer.1 = (bf16[288,768]{1,0:T(8,128)(2,1)}, f32[1,128]{1,0:T(1,128)}, bf16[288,768]{1,0:T(8,128)(2,1)}, f32[4,32]{1,0:T(4,128)}, bf16[5,4,96,384]{3,2,1,0:T(8,...) custom-call(bf16[288,768]{1,0:T(8,128)(2,1)} %bitcast.16, s32[1,288]{1,0:T(1,128)} %bitcast.20, ...), custom_call_target="tpu_custom_call" | custom-call | tf_op jit(solution)/shard_map/layer/pallas_call | solution.py:1215
  75.5 4.1 %finish.1 = (bf16[288,768]{1,0:T(8,128)(2,1)}, f32[1,4]{1,0:T(1,128)}, bf16[288,768]{1,0:T(8,128)(2,1)}, f32[4,32]{1,0:T(4,128)}, f32[96,2304]{1,0:T(8,128)}, /*...) custom-call(bf16[288,768]{1,0:T(8,128)(2,1)} %get-tuple-element.41.b, ...), custom_call_target="tpu_custom_call" | custom-call | tf_op jit(solution)/shard_map/finish/pallas_call | solution.py:1230
